TPU v7x, 128 devices: a whole 4x4x4 slice. The times are simulated.
128 devices in a mesh: slab: 16 (over z, y), lat: 8 (over x, core).
Axes of the slice: x: 4, y: 4, z: 4, core: 2. Of those that a mesh axis runs over, the one named last changes fastest.
Arguments:
- residual_blocks: float32 [4096, 2, 64, 128], P(('slab', 'lat')), may hold values from -1.5 to 1.5
- residual_slab: int32 [4096, 1], P(('slab', 'lat')), may hold values from 0 to 15; in each aligned block of 32 rows (0 to 31, 32 to 63, ...) at most 4 rows name the same one
- residual_pos: int32 [4096], P(('slab', 'lat')), may hold values from 0 to 3
- shot_ids: int32 [64], replicated, may hold values from 0 to 63, each once
- wavelet: float32 [64, 2], replicated, may hold values from -4 to 4
- down_panel: float32 [16, 8, 2, 512, 512], P('slab', 'lat'), may hold values from -1 to 1
- up_panel: float32 [16, 8, 2, 512, 512], P('slab', 'lat'), may hold values from -1 to 1
- recovery: float32 [16, 8, 2, 768, 1024], P('slab', 'lat'), may hold values from -0.109375 to 0.109375
- forward_field: float32 [16, 8, 2, 64, 1024], P('slab', 'lat'), may hold values from -3 to 3
- element_owner: int32 [1024, 1], P(('slab', 'lat')), may hold values from 0 to 15; in each aligned block of 8 rows (0 to 7, 8 to 15, ...) at most 2 rows name the same one
- element_slot: int32 [1024], P(('slab', 'lat')), may hold values from 0 to 7
Outputs:
- adjoint_trace: float32 [16, 8, 2, 64, 512], P('slab', 'lat')
- velocity_gradient: float32 [16, 8, 8, 128], P('slab', 'lat')
Inputs may be any that keep to these rules, and one draw needn't show every extreme that they name: `residual_slab`: in the 32 rows of one device no slab is named more than 4 times, a bound that some block reaches. `shot_ids`: each shot number appears once. `element_owner`: in the 8 rows of one device no slab is named more than 2 times, a bound that some block reaches.
All inputs are finite; a program needn't handle non-finite values.
Results may differ from a plain program's by a relative error of at most 0.00014.
Values sent between devices are 32-bit elements; how exact they have to be, the bound alone decides.
A program may use at most 128 MiB of HBM per device.

v0:
```python
import jax
import jax.numpy as jnp
from jax import lax
from jax.sharding import PartitionSpec as P

MBLK = 8
GCAP = 2


def shifted(block, axis, distance):
    devices = range(lax.axis_size(axis))
    route = [(i - distance, i) for i in devices if i - distance in devices]
    return lax.ppermute(block, axis, route)


def padded(cells, sides, width):
    for axis, dim in sides:
        count = lax.axis_size(axis)
        ends = count - 1
        head = lax.slice_in_dim(cells, 0, width, axis=dim)
        tail = lax.slice_in_dim(cells, cells.shape[dim] - width, cells.shape[dim], axis=dim)
        cells = jnp.concatenate(
            [
                lax.ppermute(tail, axis, [(i, (i + 1) % count) for i in range(ends)]),
                cells,
                lax.ppermute(head, axis, [((i + 1) % count, i) for i in range(ends)]),
            ],
            axis=dim,
        )
    return cells


def complex_product(vector, panel):
    value_re = vector[..., 0, :, :]
    value_im = vector[..., 1, :, :]
    panel_re = panel[..., 0, :, :]
    panel_im = panel[..., 1, :, :]
    first = jnp.matmul(value_re, panel_re, precision=lax.Precision.HIGHEST) - jnp.matmul(
        value_im, panel_im, precision=lax.Precision.HIGHEST
    )
    second = jnp.matmul(value_re, panel_im, precision=lax.Precision.HIGHEST) + jnp.matmul(
        value_im, panel_re, precision=lax.Precision.HIGHEST
    )
    return jnp.stack([first, second], axis=-3)


def slot_numbers(targets, count):
    member = (targets[:, None] == jnp.arange(count, dtype=jnp.int32)[None, :]).astype(jnp.int32)
    return jnp.sum(jnp.cumsum(member, axis=0) * member, axis=1) - 1


def body(
    residual_blocks,
    residual_slab,
    residual_pos,
    shot_ids,
    wavelet,
    down_panel,
    up_panel,
    recovery,
    forward_field,
    element_owner,
    element_slot,
):
    slab_count = lax.axis_size("slab")
    block_count = residual_blocks.shape[0]
    shots = residual_blocks.shape[2]
    width = residual_blocks.shape[3]
    trace = down_panel.shape[-1]
    places = trace // width
    targets = residual_slab[:, 0]
    capacity = block_count // 8
    where_to = targets * capacity + slot_numbers(targets, slab_count)
    outgoing = (
        jnp.zeros((slab_count * capacity, 2, shots, width), jnp.float32)
        .at[where_to]
        .set(residual_blocks)
    )
    outgoing_pos = jnp.full((slab_count * capacity,), -1, jnp.int32).at[where_to].set(residual_pos)
    arrived, arrived_pos = (
        lax.all_to_all(outgoing, "slab", split_axis=0, concat_axis=0, tiled=True),
        lax.all_to_all(outgoing_pos, "slab", split_axis=0, concat_axis=0, tiled=True),
    )
    select = (arrived_pos[:, None] == jnp.arange(places, dtype=jnp.int32)[None, :]).astype(
        jnp.float32
    )
    summed = jnp.einsum("rp,rcsw->cspw", select, arrived, precision=lax.Precision.HIGHEST)
    summed = summed.reshape(2, shots, trace)
    picker = (shot_ids[:, None] == jnp.arange(shots, dtype=jnp.int32)[None, :]).astype(jnp.float32)
    weights = jnp.dot(picker, wavelet, precision=lax.Precision.HIGHEST)
    weight_re = weights[:, 0:1]
    weight_im = weights[:, 1:2]
    sources = jnp.stack(
        [
            weight_re * summed[0] - weight_im * summed[1],
            weight_re * summed[1] + weight_im * summed[0],
        ],
        axis=0,
    )
    downward = down_panel[0, 0]
    upward = up_panel[0, 0]

    def down_turn(counter, state):
        arrived = shifted(state, "slab", 1)
        return complex_product(arrived, downward) + sources

    downs = lax.fori_loop(0, slab_count, down_turn, jnp.zeros_like(sources))

    def up_turn(counter, state):
        arrived = shifted(state, "slab", -1)
        return complex_product(arrived, upward) + downs

    ups = lax.fori_loop(0, slab_count, up_turn, jnp.zeros_like(sources))
    extended = padded(ups, (("lat", 2),), width)
    interior = complex_product(extended, recovery[0, 0])
    gradient = jnp.sum(forward_field[0, 0] * interior, axis=(0, 1)) * shots ** (-0.5)
    pieces = gradient.reshape(-1, width)
    owners = element_owner[:, 0]
    where_to = owners * GCAP + slot_numbers(owners, slab_count)
    outgoing = jnp.zeros((slab_count * GCAP, width), jnp.float32).at[where_to].set(pieces)
    outgoing_slot = jnp.full((slab_count * GCAP,), -1, jnp.int32).at[where_to].set(element_slot)
    arrived, arrived_slot = (
        lax.all_to_all(outgoing, "slab", split_axis=0, concat_axis=0, tiled=True),
        lax.all_to_all(outgoing_slot, "slab", split_axis=0, concat_axis=0, tiled=True),
    )
    select = (arrived_slot[:, None] == jnp.arange(MBLK, dtype=jnp.int32)[None, :]).astype(
        jnp.float32
    )
    model = jnp.dot(select.T, arrived, precision=lax.Precision.HIGHEST)
    return (ups[None, None], model[None, None])


def solution(mesh):
    placed = (
        P(("slab", "lat"), None, None, None),
        P(("slab", "lat"), None),
        P(("slab", "lat")),
        P(),
        P(),
        P("slab", "lat", None, None, None),
        P("slab", "lat", None, None, None),
        P("slab", "lat", None, None, None),
        P("slab", "lat", None, None, None),
        P(("slab", "lat"), None),
        P(("slab", "lat")),
    )
    return jax.shard_map(
        body,
        mesh=mesh,
        in_specs=placed,
        out_specs=(P("slab", "lat", None, None, None), P("slab", "lat", None, None)),
        check_vma=False,
    )
```

profile of v0, /device:TPU:1, one launch (start us, length us, event | category | flops | bytes accessed | tf_op | source)
XLA Modules:
  0.0 629.4 jit_solution(8729910622789838561)
XLA Ops:
  4.6 8.6 %all-to-all-start.1 = ((s32[16,4,1]{1,2,0:T(1,128)}), s32[16,4,1]{1,2,0:T(1,128)S(1)}, u32[]{:S(2)}, u32[]{:S(2)}) async-start(s32[16,4,1]{1,2,0:T(1,128)} %bitcast.6), calls=%async_computation.1 | async-start | bytes 16384 | tf_op jit(solution)/shard_map/all_to_all | solution.py:82
  15.7 5.4 scatter_fusion
  21.1 6.9 %all-to-all-start = ((f32[64,2,64,128]{3,2,1,0:T(8,128)}), f32[64,2,64,128]{3,2,1,0:T(8,128)}, u32[]{:S(2)}, u32[]{:S(2)}) async-start(f32[64,2,64,128]{3,2,1,0:T(8,128)} %scatter_fusion), calls=%async_computation | async-start | bytes 8388608 | tf_op jit(solution)/shard_map/all_to_all | solution.py:81
  29.7 59.1 %all-to-all-done = f32[64,2,64,128]{3,2,1,0:T(8,128)} async-done(((f32[64,2,64,128]{3,2,1,0:T(8,128)}), f32[64,2,64,128]{3,2,1,0:T(8,128)}, u32[]{:S(2)}, u32[]{:S(2)}) %all-to-all-start) | async-done | bytes 4194336 | tf_op jit(solution)/shard_map/all_to_all | solution.py:81
  88.8 5.8 fusion.44
  94.8 192.6 %while.22 = (s32[]{:T(128)}, f32[2,64,512]{2,1,0:T(8,128)S(1)}, f32[2,512,512]{2,1,0:T(8,128)S(1)}, f32[2,64,512]{2,1,0:T(8,128)S(1)}, s32[]{:T(128)}, /*index=5*/s32[]{:T(128)}) while((s32[]{:T(128)}, f32[2,64,512]{2,1,0:T(8,128)S(1)}, f32[2,512,512]{2,1,0:T(8,128)S(1)}, f32[2,64,512]{2,1,0:T(8,128)S(1)}, s32[]{:T(128)}, ...), condition=%wide.region_5.6_spmd.clone, body=%wide.region_4.5_spmd.clone.sunk | while | flops 805568512 | bytes 7864439 | solution.py:107
  102.9 4.1 collective-permute-start
  123.6 3.8 collective-permute-start
  144.1 5.6 collective-permute-start
  156.1 5.9 collective-permute-start
  168.4 5.9 collective-permute-start
  180.8 5.9 collective-permute-start
  193.6 6.2 collective-permute-start
  199.8 4.9 collective-permute-done
  207.8 6.7 %collective-permute-start = (f32[2,64,512]{2,1,0:T(8,128)S(1)}, f32[2,64,512]{2,1,0:T(8,128)S(1)}, u32[]{:S(2)}, u32[]{:S(2)}) collective-permute-start(f32[2,64,512]{2,1,0:T(8,128)S(1)} %broadcast_select_fusion.4), channel_id=1, source_target_pairs={{0,8},{8,16},{16,24},{24,32},{32,40},{40,48},{48,56},{56,64},{64,7... | collective-permute-start | bytes 786440 | tf_op jit(solution)/shard_map/while/body/eval_jaxpr/ppermute | solution.py:13
  214.5 6.1 collective-permute-done
  223.7 6.3 %collective-permute-start = (f32[2,64,512]{2,1,0:T(8,128)S(1)}, f32[2,64,512]{2,1,0:T(8,128)S(1)}, u32[]{:S(2)}, u32[]{:S(2)}) collective-permute-start(f32[2,64,512]{2,1,0:T(8,128)S(1)} %broadcast_select_fusion.4), channel_id=1, source_target_pairs={{0,8},{8,16},{16,24},{24,32},{32,40},{40,48},{48,56},{56,64},{64,7... | collective-permute-start | bytes 786440 | tf_op jit(solution)/shard_map/while/body/eval_jaxpr/ppermute | solution.py:13
  230.0 5.0 collective-permute-done
  238.2 5.6 collective-permute-start
  243.8 3.9 collective-permute-done
  250.8 5.0 collective-permute-start
  262.2 6.2 collective-permute-start
  274.8 6.2 collective-permute-start
  287.4 250.2 %while.23 = (s32[]{:T(128)}, f32[2,64,512]{2,1,0:T(8,128)S(1)}, f32[2,512,512]{2,1,0:T(8,128)}, f32[2,64,512]{2,1,0:T(8,128)S(1)}, s32[]{:T(128)}, /*index=5*/s32[]{:T(128)}) while((s32[]{:T(128)}, f32[2,64,512]{2,1,0:T(8,128)S(1)}, f32[2,512,512]{2,1,0:T(8,128)}, f32[2,64,512]{2,1,0:T(8,128)S(1)}, s32[]{:T(128)}, ...), condition=%wide.region_7.8_spmd.clone, body=%wide.region_6.7_spmd.clone.sunk | while | flops 805568512 | bytes 16253075 | solution.py:113
  288.9 8.7 %collective-permute-done.1 = f32[2,64,512]{2,1,0:T(8,128)S(1)} collective-permute-done((f32[2,64,512]{2,1,0:T(8,128)S(1)}, f32[2,64,512]{2,1,0:T(8,128)S(1)}, u32[]{:S(2)}, u32[]{:S(2)}) %collective-permute-start.1) | collective-permute-done | bytes 262176 | tf_op jit(solution)/shard_map/while/body/eval_jaxpr/ppermute | solution.py:13
  304.6 8.4 %collective-permute-done.1 = f32[2,64,512]{2,1,0:T(8,128)S(1)} collective-permute-done((f32[2,64,512]{2,1,0:T(8,128)S(1)}, f32[2,64,512]{2,1,0:T(8,128)S(1)}, u32[]{:S(2)}, u32[]{:S(2)}) %collective-permute-start.1) | collective-permute-done | bytes 262176 | tf_op jit(solution)/shard_map/while/body/eval_jaxpr/ppermute | solution.py:13
  320.0 8.4 %collective-permute-done.1 = f32[2,64,512]{2,1,0:T(8,128)S(1)} collective-permute-done((f32[2,64,512]{2,1,0:T(8,128)S(1)}, f32[2,64,512]{2,1,0:T(8,128)S(1)}, u32[]{:S(2)}, u32[]{:S(2)}) %collective-permute-start.1) | collective-permute-done | bytes 262176 | tf_op jit(solution)/shard_map/while/body/eval_jaxpr/ppermute | solution.py:13
  335.4 8.4 %collective-permute-done.1 = f32[2,64,512]{2,1,0:T(8,128)S(1)} collective-permute-done((f32[2,64,512]{2,1,0:T(8,128)S(1)}, f32[2,64,512]{2,1,0:T(8,128)S(1)}, u32[]{:S(2)}, u32[]{:S(2)}) %collective-permute-start.1) | collective-permute-done | bytes 262176 | tf_op jit(solution)/shard_map/while/body/eval_jaxpr/ppermute | solution.py:13
  350.7 7.9 %collective-permute-done.1 = f32[2,64,512]{2,1,0:T(8,128)S(1)} collective-permute-done((f32[2,64,512]{2,1,0:T(8,128)S(1)}, f32[2,64,512]{2,1,0:T(8,128)S(1)}, u32[]{:S(2)}, u32[]{:S(2)}) %collective-permute-start.1) | collective-permute-done | bytes 262176 | tf_op jit(solution)/shard_map/while/body/eval_jaxpr/ppermute | solution.py:13
  365.7 7.9 %collective-permute-done.1 = f32[2,64,512]{2,1,0:T(8,128)S(1)} collective-permute-done((f32[2,64,512]{2,1,0:T(8,128)S(1)}, f32[2,64,512]{2,1,0:T(8,128)S(1)}, u32[]{:S(2)}, u32[]{:S(2)}) %collective-permute-start.1) | collective-permute-done | bytes 262176 | tf_op jit(solution)/shard_map/while/body/eval_jaxpr/ppermute | solution.py:13
  380.6 7.9 %collective-permute-done.1 = f32[2,64,512]{2,1,0:T(8,128)S(1)} collective-permute-done((f32[2,64,512]{2,1,0:T(8,128)S(1)}, f32[2,64,512]{2,1,0:T(8,128)S(1)}, u32[]{:S(2)}, u32[]{:S(2)}) %collective-permute-start.1) | collective-permute-done | bytes 262176 | tf_op jit(solution)/shard_map/while/body/eval_jaxpr/ppermute | solution.py:13
  395.5 7.9 %collective-permute-done.1 = f32[2,64,512]{2,1,0:T(8,128)S(1)} collective-permute-done((f32[2,64,512]{2,1,0:T(8,128)S(1)}, f32[2,64,512]{2,1,0:T(8,128)S(1)}, u32[]{:S(2)}, u32[]{:S(2)}) %collective-permute-start.1) | collective-permute-done | bytes 262176 | tf_op jit(solution)/shard_map/while/body/eval_jaxpr/ppermute | solution.py:13
  410.5 7.9 %collective-permute-done.1 = f32[2,64,512]{2,1,0:T(8,128)S(1)} collective-permute-done((f32[2,64,512]{2,1,0:T(8,128)S(1)}, f32[2,64,512]{2,1,0:T(8,128)S(1)}, u32[]{:S(2)}, u32[]{:S(2)}) %collective-permute-start.1) | collective-permute-done | bytes 262176 | tf_op jit(solution)/shard_map/while/body/eval_jaxpr/ppermute | solution.py:13
  425.4 8.1 %collective-permute-done.1 = f32[2,64,512]{2,1,0:T(8,128)S(1)} collective-permute-done((f32[2,64,512]{2,1,0:T(8,128)S(1)}, f32[2,64,512]{2,1,0:T(8,128)S(1)}, u32[]{:S(2)}, u32[]{:S(2)}) %collective-permute-start.1) | collective-permute-done | bytes 262176 | tf_op jit(solution)/shard_map/while/body/eval_jaxpr/ppermute | solution.py:13
  440.5 9.5 %collective-permute-done.1 = f32[2,64,512]{2,1,0:T(8,128)S(1)} collective-permute-done((f32[2,64,512]{2,1,0:T(8,128)S(1)}, f32[2,64,512]{2,1,0:T(8,128)S(1)}, u32[]{:S(2)}, u32[]{:S(2)}) %collective-permute-start.1) | collective-permute-done | bytes 262176 | tf_op jit(solution)/shard_map/while/body/eval_jaxpr/ppermute | solution.py:13
  457.1 11.0 %collective-permute-done.1 = f32[2,64,512]{2,1,0:T(8,128)S(1)} collective-permute-done((f32[2,64,512]{2,1,0:T(8,128)S(1)}, f32[2,64,512]{2,1,0:T(8,128)S(1)}, u32[]{:S(2)}, u32[]{:S(2)}) %collective-permute-start.1) | collective-permute-done | bytes 262176 | tf_op jit(solution)/shard_map/while/body/eval_jaxpr/ppermute | solution.py:13
  475.0 11.5 %collective-permute-done.1 = f32[2,64,512]{2,1,0:T(8,128)S(1)} collective-permute-done((f32[2,64,512]{2,1,0:T(8,128)S(1)}, f32[2,64,512]{2,1,0:T(8,128)S(1)}, u32[]{:S(2)}, u32[]{:S(2)}) %collective-permute-start.1) | collective-permute-done | bytes 262176 | tf_op jit(solution)/shard_map/while/body/eval_jaxpr/ppermute | solution.py:13
  493.6 9.6 %collective-permute-done.1 = f32[2,64,512]{2,1,0:T(8,128)S(1)} collective-permute-done((f32[2,64,512]{2,1,0:T(8,128)S(1)}, f32[2,64,512]{2,1,0:T(8,128)S(1)}, u32[]{:S(2)}, u32[]{:S(2)}) %collective-permute-start.1) | collective-permute-done | bytes 262176 | tf_op jit(solution)/shard_map/while/body/eval_jaxpr/ppermute | solution.py:13
  510.1 8.0 %collective-permute-done.1 = f32[2,64,512]{2,1,0:T(8,128)S(1)} collective-permute-done((f32[2,64,512]{2,1,0:T(8,128)S(1)}, f32[2,64,512]{2,1,0:T(8,128)S(1)}, u32[]{:S(2)}, u32[]{:S(2)}) %collective-permute-start.1) | collective-permute-done | bytes 262176 | tf_op jit(solution)/shard_map/while/body/eval_jaxpr/ppermute | solution.py:13
  525.1 7.1 %collective-permute-done.1 = f32[2,64,512]{2,1,0:T(8,128)S(1)} collective-permute-done((f32[2,64,512]{2,1,0:T(8,128)S(1)}, f32[2,64,512]{2,1,0:T(8,128)S(1)}, u32[]{:S(2)}, u32[]{:S(2)}) %collective-permute-start.1) | collective-permute-done | bytes 262176 | tf_op jit(solution)/shard_map/while/body/eval_jaxpr/ppermute | solution.py:13
  537.7 39.0 %collective-permute-start.2 = (f32[2,64,128]{2,1,0:T(8,128)S(1)}, f32[2,64,128]{2,1,0:T(8,128)S(1)}, u32[]{:S(2)}, u32[]{:S(2)}) collective-permute-start(f32[2,64,128]{2,1,0:T(8,128)S(1)} %get-tuple-element.97), channel_id=1, source_target_pairs={{0,1},{1,2},{2,3},{3,4},{4,5},{5,6},{6,7},{8,9},{9,10},{10,11},{11... | collective-permute-start | bytes 196616 | tf_op jit(solution)/shard_map/ppermute | solution.py:24
  578.2 14.8 %all-to-all-start.2 = ((s32[16,2,1]{1,2,0:T(1,128)}), s32[16,2,1]{1,2,0:T(1,128)S(1)}, u32[]{:S(2)}, u32[]{:S(2)}) async-start(s32[16,2,1]{1,2,0:T(1,128)} %bitcast.15), calls=%async_computation.2 | async-start | bytes 16384 | tf_op jit(solution)/shard_map/all_to_all | solution.py:124
  598.5 3.9 fusion.28
  602.4 3.9 fusion.30
  606.3 4.0 fusion.50
  610.3 3.9 fusion.47
  615.5 6.6 %all-to-all-start.3 = ((f32[16,2,128]{2,1,0:T(2,128)}), f32[16,2,128]{2,1,0:T(2,128)S(1)}, u32[]{:S(2)}, u32[]{:S(2)}) async-start(f32[16,2,128]{2,1,0:T(2,128)} %bitcast.24), calls=%async_computation.3 | async-start | bytes 32768 | tf_op jit(solution)/shard_map/all_to_all | solution.py:123
  622.8 5.8 all-to-all-done.3
  (308 shorter events, 227.7 us)
Async XLA Ops:
  0.6 27.6 %copy-start = (f32[64,2]{0,1:T(2,128)S(1)}, f32[64,2]{0,1:T(2,128)}, u32[]{:S(2)}) copy-start(f32[64,2]{0,1:T(2,128)} %param.19) | copy-start | bytes 1540
  0.6 15.0 %copy-start.4 = (f32[32,2,64,128]{3,2,1,0:T(8,128)S(1)}, f32[32,2,64,128]{3,2,1,0:T(8,128)}, u32[]{:S(2)}) copy-start(f32[32,2,64,128]{3,2,1,0:T(8,128)} %param.15) | copy-start | bytes 6291460
  4.6 16.5 %all-to-all-start.1 = ((s32[16,4,1]{1,2,0:T(1,128)}), s32[16,4,1]{1,2,0:T(1,128)S(1)}, u32[]{:S(2)}, u32[]{:S(2)}) async-start(s32[16,4,1]{1,2,0:T(1,128)} %bitcast.6), calls=%async_computation.1 | async-start | bytes 16384 | tf_op jit(solution)/shard_map/all_to_all | solution.py:82
  21.1 67.7 %all-to-all-start = ((f32[64,2,64,128]{3,2,1,0:T(8,128)}), f32[64,2,64,128]{3,2,1,0:T(8,128)}, u32[]{:S(2)}, u32[]{:S(2)}) async-start(f32[64,2,64,128]{3,2,1,0:T(8,128)} %scatter_fusion), calls=%async_computation | async-start | bytes 8388608 | tf_op jit(solution)/shard_map/all_to_all | solution.py:81
  29.7 65.1 %copy-start.1 = (f32[1,1,2,512,512]{4,3,2,1,0:T(8,128)S(1)}, f32[1,1,2,512,512]{4,3,2,1,0:T(8,128)}, u32[]{:S(2)}) copy-start(f32[1,1,2,512,512]{4,3,2,1,0:T(8,128)} %param.20) | copy-start | bytes 6291460
  94.9 4.9 collective-permute-start
  102.9 7.4 %collective-permute-start = (f32[2,64,512]{2,1,0:T(8,128)S(1)}, f32[2,64,512]{2,1,0:T(8,128)S(1)}, u32[]{:S(2)}, u32[]{:S(2)}) collective-permute-start(f32[2,64,512]{2,1,0:T(8,128)S(1)} %broadcast_select_fusion.4), channel_id=1, source_target_pairs={{0,8},{8,16},{16,24},{24,32},{32,40},{40,48},{48,56},{56,64},{64,7... | collective-permute-start | bytes 786440 | tf_op jit(solution)/shard_map/while/body/eval_jaxpr/ppermute | solution.py:13
  113.4 7.1 %collective-permute-start = (f32[2,64,512]{2,1,0:T(8,128)S(1)}, f32[2,64,512]{2,1,0:T(8,128)S(1)}, u32[]{:S(2)}, u32[]{:S(2)}) collective-permute-start(f32[2,64,512]{2,1,0:T(8,128)S(1)} %broadcast_select_fusion.4), channel_id=1, source_target_pairs={{0,8},{8,16},{16,24},{24,32},{32,40},{40,48},{48,56},{56,64},{64,7... | collective-permute-start | bytes 786440 | tf_op jit(solution)/shard_map/while/body/eval_jaxpr/ppermute | solution.py:13
  123.6 7.1 %collective-permute-start = (f32[2,64,512]{2,1,0:T(8,128)S(1)}, f32[2,64,512]{2,1,0:T(8,128)S(1)}, u32[]{:S(2)}, u32[]{:S(2)}) collective-permute-start(f32[2,64,512]{2,1,0:T(8,128)S(1)} %broadcast_select_fusion.4), channel_id=1, source_target_pairs={{0,8},{8,16},{16,24},{24,32},{32,40},{40,48},{48,56},{56,64},{64,7... | collective-permute-start | bytes 786440 | tf_op jit(solution)/shard_map/while/body/eval_jaxpr/ppermute | solution.py:13
  133.9 7.1 %collective-permute-start = (f32[2,64,512]{2,1,0:T(8,128)S(1)}, f32[2,64,512]{2,1,0:T(8,128)S(1)}, u32[]{:S(2)}, u32[]{:S(2)}) collective-permute-start(f32[2,64,512]{2,1,0:T(8,128)S(1)} %broadcast_select_fusion.4), channel_id=1, source_target_pairs={{0,8},{8,16},{16,24},{24,32},{32,40},{40,48},{48,56},{56,64},{64,7... | collective-permute-start | bytes 786440 | tf_op jit(solution)/shard_map/while/body/eval_jaxpr/ppermute | solution.py:13
  144.1 8.9 %collective-permute-start = (f32[2,64,512]{2,1,0:T(8,128)S(1)}, f32[2,64,512]{2,1,0:T(8,128)S(1)}, u32[]{:S(2)}, u32[]{:S(2)}) collective-permute-start(f32[2,64,512]{2,1,0:T(8,128)S(1)} %broadcast_select_fusion.4), channel_id=1, source_target_pairs={{0,8},{8,16},{16,24},{24,32},{32,40},{40,48},{48,56},{56,64},{64,7... | collective-permute-start | bytes 786440 | tf_op jit(solution)/shard_map/while/body/eval_jaxpr/ppermute | solution.py:13
  156.1 9.2 %collective-permute-start = (f32[2,64,512]{2,1,0:T(8,128)S(1)}, f32[2,64,512]{2,1,0:T(8,128)S(1)}, u32[]{:S(2)}, u32[]{:S(2)}) collective-permute-start(f32[2,64,512]{2,1,0:T(8,128)S(1)} %broadcast_select_fusion.4), channel_id=1, source_target_pairs={{0,8},{8,16},{16,24},{24,32},{32,40},{40,48},{48,56},{56,64},{64,7... | collective-permute-start | bytes 786440 | tf_op jit(solution)/shard_map/while/body/eval_jaxpr/ppermute | solution.py:13
  168.4 9.2 %collective-permute-start = (f32[2,64,512]{2,1,0:T(8,128)S(1)}, f32[2,64,512]{2,1,0:T(8,128)S(1)}, u32[]{:S(2)}, u32[]{:S(2)}) collective-permute-start(f32[2,64,512]{2,1,0:T(8,128)S(1)} %broadcast_select_fusion.4), channel_id=1, source_target_pairs={{0,8},{8,16},{16,24},{24,32},{32,40},{40,48},{48,56},{56,64},{64,7... | collective-permute-start | bytes 786440 | tf_op jit(solution)/shard_map/while/body/eval_jaxpr/ppermute | solution.py:13
  180.8 9.7 %collective-permute-start = (f32[2,64,512]{2,1,0:T(8,128)S(1)}, f32[2,64,512]{2,1,0:T(8,128)S(1)}, u32[]{:S(2)}, u32[]{:S(2)}) collective-permute-start(f32[2,64,512]{2,1,0:T(8,128)S(1)} %broadcast_select_fusion.4), channel_id=1, source_target_pairs={{0,8},{8,16},{16,24},{24,32},{32,40},{40,48},{48,56},{56,64},{64,7... | collective-permute-start | bytes 786440 | tf_op jit(solution)/shard_map/while/body/eval_jaxpr/ppermute | solution.py:13
  193.6 11.1 %collective-permute-start = (f32[2,64,512]{2,1,0:T(8,128)S(1)}, f32[2,64,512]{2,1,0:T(8,128)S(1)}, u32[]{:S(2)}, u32[]{:S(2)}) collective-permute-start(f32[2,64,512]{2,1,0:T(8,128)S(1)} %broadcast_select_fusion.4), channel_id=1, source_target_pairs={{0,8},{8,16},{16,24},{24,32},{32,40},{40,48},{48,56},{56,64},{64,7... | collective-permute-start | bytes 786440 | tf_op jit(solution)/shard_map/while/body/eval_jaxpr/ppermute | solution.py:13
  207.8 12.8 %collective-permute-start = (f32[2,64,512]{2,1,0:T(8,128)S(1)}, f32[2,64,512]{2,1,0:T(8,128)S(1)}, u32[]{:S(2)}, u32[]{:S(2)}) collective-permute-start(f32[2,64,512]{2,1,0:T(8,128)S(1)} %broadcast_select_fusion.4), channel_id=1, source_target_pairs={{0,8},{8,16},{16,24},{24,32},{32,40},{40,48},{48,56},{56,64},{64,7... | collective-permute-start | bytes 786440 | tf_op jit(solution)/shard_map/while/body/eval_jaxpr/ppermute | solution.py:13
  223.7 11.4 %collective-permute-start = (f32[2,64,512]{2,1,0:T(8,128)S(1)}, f32[2,64,512]{2,1,0:T(8,128)S(1)}, u32[]{:S(2)}, u32[]{:S(2)}) collective-permute-start(f32[2,64,512]{2,1,0:T(8,128)S(1)} %broadcast_select_fusion.4), channel_id=1, source_target_pairs={{0,8},{8,16},{16,24},{24,32},{32,40},{40,48},{48,56},{56,64},{64,7... | collective-permute-start | bytes 786440 | tf_op jit(solution)/shard_map/while/body/eval_jaxpr/ppermute | solution.py:13
  238.2 9.5 %collective-permute-start = (f32[2,64,512]{2,1,0:T(8,128)S(1)}, f32[2,64,512]{2,1,0:T(8,128)S(1)}, u32[]{:S(2)}, u32[]{:S(2)}) collective-permute-start(f32[2,64,512]{2,1,0:T(8,128)S(1)} %broadcast_select_fusion.4), channel_id=1, source_target_pairs={{0,8},{8,16},{16,24},{24,32},{32,40},{40,48},{48,56},{56,64},{64,7... | collective-permute-start | bytes 786440 | tf_op jit(solution)/shard_map/while/body/eval_jaxpr/ppermute | solution.py:13
  250.8 8.3 %collective-permute-start = (f32[2,64,512]{2,1,0:T(8,128)S(1)}, f32[2,64,512]{2,1,0:T(8,128)S(1)}, u32[]{:S(2)}, u32[]{:S(2)}) collective-permute-start(f32[2,64,512]{2,1,0:T(8,128)S(1)} %broadcast_select_fusion.4), channel_id=1, source_target_pairs={{0,8},{8,16},{16,24},{24,32},{32,40},{40,48},{48,56},{56,64},{64,7... | collective-permute-start | bytes 786440 | tf_op jit(solution)/shard_map/while/body/eval_jaxpr/ppermute | solution.py:13
  262.2 9.5 %collective-permute-start = (f32[2,64,512]{2,1,0:T(8,128)S(1)}, f32[2,64,512]{2,1,0:T(8,128)S(1)}, u32[]{:S(2)}, u32[]{:S(2)}) collective-permute-start(f32[2,64,512]{2,1,0:T(8,128)S(1)} %broadcast_select_fusion.4), channel_id=1, source_target_pairs={{0,8},{8,16},{16,24},{24,32},{32,40},{40,48},{48,56},{56,64},{64,7... | collective-permute-start | bytes 786440 | tf_op jit(solution)/shard_map/while/body/eval_jaxpr/ppermute | solution.py:13
  274.8 9.5 %collective-permute-start = (f32[2,64,512]{2,1,0:T(8,128)S(1)}, f32[2,64,512]{2,1,0:T(8,128)S(1)}, u32[]{:S(2)}, u32[]{:S(2)}) collective-permute-start(f32[2,64,512]{2,1,0:T(8,128)S(1)} %broadcast_select_fusion.4), channel_id=1, source_target_pairs={{0,8},{8,16},{16,24},{24,32},{32,40},{40,48},{48,56},{56,64},{64,7... | collective-permute-start | bytes 786440 | tf_op jit(solution)/shard_map/while/body/eval_jaxpr/ppermute | solution.py:13
  287.4 14.1 %copy-start.2 = (f32[2,512,512]{2,1,0:T(8,128)S(1)}, f32[2,512,512]{2,1,0:T(8,128)}, u32[]{:S(2)}) copy-start(f32[2,512,512]{2,1,0:T(8,128)} %get-tuple-element.184) | copy-start | bytes 6291460 | tf_op jit(solution)/shard_map/while
  287.5 10.1 %collective-permute-start.1 = (f32[2,64,512]{2,1,0:T(8,128)S(1)}, f32[2,64,512]{2,1,0:T(8,128)S(1)}, u32[]{:S(2)}, u32[]{:S(2)}) collective-permute-start(f32[2,64,512]{2,1,0:T(8,128)S(1)} %broadcast_select_fusion.5), channel_id=1, source_target_pairs={{8,0},{16,8},{24,16},{32,24},{40,32},{48,40},{56,48},{64,56},{72,6... | collective-permute-start | bytes 786440 | tf_op jit(solution)/shard_map/while/body/eval_jaxpr/ppermute | solution.py:13
  303.1 13.8 %copy-start.2 = (f32[2,512,512]{2,1,0:T(8,128)S(1)}, f32[2,512,512]{2,1,0:T(8,128)}, u32[]{:S(2)}) copy-start(f32[2,512,512]{2,1,0:T(8,128)} %get-tuple-element.184) | copy-start | bytes 6291460 | tf_op jit(solution)/shard_map/while
  303.2 9.8 %collective-permute-start.1 = (f32[2,64,512]{2,1,0:T(8,128)S(1)}, f32[2,64,512]{2,1,0:T(8,128)S(1)}, u32[]{:S(2)}, u32[]{:S(2)}) collective-permute-start(f32[2,64,512]{2,1,0:T(8,128)S(1)} %broadcast_select_fusion.5), channel_id=1, source_target_pairs={{8,0},{16,8},{24,16},{32,24},{40,32},{48,40},{56,48},{64,56},{72,6... | collective-permute-start | bytes 786440 | tf_op jit(solution)/shard_map/while/body/eval_jaxpr/ppermute | solution.py:13
  318.5 9.8 %collective-permute-start.1 = (f32[2,64,512]{2,1,0:T(8,128)S(1)}, f32[2,64,512]{2,1,0:T(8,128)S(1)}, u32[]{:S(2)}, u32[]{:S(2)}) collective-permute-start(f32[2,64,512]{2,1,0:T(8,128)S(1)} %broadcast_select_fusion.5), channel_id=1, source_target_pairs={{8,0},{16,8},{24,16},{32,24},{40,32},{48,40},{56,48},{64,56},{72,6... | collective-permute-start | bytes 786440 | tf_op jit(solution)/shard_map/while/body/eval_jaxpr/ppermute | solution.py:13
  333.9 9.8 %collective-permute-start.1 = (f32[2,64,512]{2,1,0:T(8,128)S(1)}, f32[2,64,512]{2,1,0:T(8,128)S(1)}, u32[]{:S(2)}, u32[]{:S(2)}) collective-permute-start(f32[2,64,512]{2,1,0:T(8,128)S(1)} %broadcast_select_fusion.5), channel_id=1, source_target_pairs={{8,0},{16,8},{24,16},{32,24},{40,32},{48,40},{56,48},{64,56},{72,6... | collective-permute-start | bytes 786440 | tf_op jit(solution)/shard_map/while/body/eval_jaxpr/ppermute | solution.py:13
  349.3 9.4 %collective-permute-start.1 = (f32[2,64,512]{2,1,0:T(8,128)S(1)}, f32[2,64,512]{2,1,0:T(8,128)S(1)}, u32[]{:S(2)}, u32[]{:S(2)}) collective-permute-start(f32[2,64,512]{2,1,0:T(8,128)S(1)} %broadcast_select_fusion.5), channel_id=1, source_target_pairs={{8,0},{16,8},{24,16},{32,24},{40,32},{48,40},{56,48},{64,56},{72,6... | collective-permute-start | bytes 786440 | tf_op jit(solution)/shard_map/while/body/eval_jaxpr/ppermute | solution.py:13
  364.2 9.4 %collective-permute-start.1 = (f32[2,64,512]{2,1,0:T(8,128)S(1)}, f32[2,64,512]{2,1,0:T(8,128)S(1)}, u32[]{:S(2)}, u32[]{:S(2)}) collective-permute-start(f32[2,64,512]{2,1,0:T(8,128)S(1)} %broadcast_select_fusion.5), channel_id=1, source_target_pairs={{8,0},{16,8},{24,16},{32,24},{40,32},{48,40},{56,48},{64,56},{72,6... | collective-permute-start | bytes 786440 | tf_op jit(solution)/shard_map/while/body/eval_jaxpr/ppermute | solution.py:13
  379.2 9.4 %collective-permute-start.1 = (f32[2,64,512]{2,1,0:T(8,128)S(1)}, f32[2,64,512]{2,1,0:T(8,128)S(1)}, u32[]{:S(2)}, u32[]{:S(2)}) collective-permute-start(f32[2,64,512]{2,1,0:T(8,128)S(1)} %broadcast_select_fusion.5), channel_id=1, source_target_pairs={{8,0},{16,8},{24,16},{32,24},{40,32},{48,40},{56,48},{64,56},{72,6... | collective-permute-start | bytes 786440 | tf_op jit(solution)/shard_map/while/body/eval_jaxpr/ppermute | solution.py:13
  394.1 9.4 %collective-permute-start.1 = (f32[2,64,512]{2,1,0:T(8,128)S(1)}, f32[2,64,512]{2,1,0:T(8,128)S(1)}, u32[]{:S(2)}, u32[]{:S(2)}) collective-permute-start(f32[2,64,512]{2,1,0:T(8,128)S(1)} %broadcast_select_fusion.5), channel_id=1, source_target_pairs={{8,0},{16,8},{24,16},{32,24},{40,32},{48,40},{56,48},{64,56},{72,6... | collective-permute-start | bytes 786440 | tf_op jit(solution)/shard_map/while/body/eval_jaxpr/ppermute | solution.py:13
  409.0 9.4 %collective-permute-start.1 = (f32[2,64,512]{2,1,0:T(8,128)S(1)}, f32[2,64,512]{2,1,0:T(8,128)S(1)}, u32[]{:S(2)}, u32[]{:S(2)}) collective-permute-start(f32[2,64,512]{2,1,0:T(8,128)S(1)} %broadcast_select_fusion.5), channel_id=1, source_target_pairs={{8,0},{16,8},{24,16},{32,24},{40,32},{48,40},{56,48},{64,56},{72,6... | collective-permute-start | bytes 786440 | tf_op jit(solution)/shard_map/while/body/eval_jaxpr/ppermute | solution.py:13
  424.0 9.6 %collective-permute-start.1 = (f32[2,64,512]{2,1,0:T(8,128)S(1)}, f32[2,64,512]{2,1,0:T(8,128)S(1)}, u32[]{:S(2)}, u32[]{:S(2)}) collective-permute-start(f32[2,64,512]{2,1,0:T(8,128)S(1)} %broadcast_select_fusion.5), channel_id=1, source_target_pairs={{8,0},{16,8},{24,16},{32,24},{40,32},{48,40},{56,48},{64,56},{72,6... | collective-permute-start | bytes 786440 | tf_op jit(solution)/shard_map/while/body/eval_jaxpr/ppermute | solution.py:13
  439.1 15.0 %copy-start.2 = (f32[2,512,512]{2,1,0:T(8,128)S(1)}, f32[2,512,512]{2,1,0:T(8,128)}, u32[]{:S(2)}) copy-start(f32[2,512,512]{2,1,0:T(8,128)} %get-tuple-element.184) | copy-start | bytes 6291460 | tf_op jit(solution)/shard_map/while
  439.1 11.0 %collective-permute-start.1 = (f32[2,64,512]{2,1,0:T(8,128)S(1)}, f32[2,64,512]{2,1,0:T(8,128)S(1)}, u32[]{:S(2)}, u32[]{:S(2)}) collective-permute-start(f32[2,64,512]{2,1,0:T(8,128)S(1)} %broadcast_select_fusion.5), channel_id=1, source_target_pairs={{8,0},{16,8},{24,16},{32,24},{40,32},{48,40},{56,48},{64,56},{72,6... | collective-permute-start | bytes 786440 | tf_op jit(solution)/shard_map/while/body/eval_jaxpr/ppermute | solution.py:13
  455.6 16.4 %copy-start.2 = (f32[2,512,512]{2,1,0:T(8,128)S(1)}, f32[2,512,512]{2,1,0:T(8,128)}, u32[]{:S(2)}) copy-start(f32[2,512,512]{2,1,0:T(8,128)} %get-tuple-element.184) | copy-start | bytes 6291460 | tf_op jit(solution)/shard_map/while
  455.6 12.4 %collective-permute-start.1 = (f32[2,64,512]{2,1,0:T(8,128)S(1)}, f32[2,64,512]{2,1,0:T(8,128)S(1)}, u32[]{:S(2)}, u32[]{:S(2)}) collective-permute-start(f32[2,64,512]{2,1,0:T(8,128)S(1)} %broadcast_select_fusion.5), channel_id=1, source_target_pairs={{8,0},{16,8},{24,16},{32,24},{40,32},{48,40},{56,48},{64,56},{72,6... | collective-permute-start | bytes 786440 | tf_op jit(solution)/shard_map/while/body/eval_jaxpr/ppermute | solution.py:13
  473.6 16.9 %copy-start.2 = (f32[2,512,512]{2,1,0:T(8,128)S(1)}, f32[2,512,512]{2,1,0:T(8,128)}, u32[]{:S(2)}) copy-start(f32[2,512,512]{2,1,0:T(8,128)} %get-tuple-element.184) | copy-start | bytes 6291460 | tf_op jit(solution)/shard_map/while
  473.6 12.9 %collective-permute-start.1 = (f32[2,64,512]{2,1,0:T(8,128)S(1)}, f32[2,64,512]{2,1,0:T(8,128)S(1)}, u32[]{:S(2)}, u32[]{:S(2)}) collective-permute-start(f32[2,64,512]{2,1,0:T(8,128)S(1)} %broadcast_select_fusion.5), channel_id=1, source_target_pairs={{8,0},{16,8},{24,16},{32,24},{40,32},{48,40},{56,48},{64,56},{72,6... | collective-permute-start | bytes 786440 | tf_op jit(solution)/shard_map/while/body/eval_jaxpr/ppermute | solution.py:13
  492.1 15.0 %copy-start.2 = (f32[2,512,512]{2,1,0:T(8,128)S(1)}, f32[2,512,512]{2,1,0:T(8,128)}, u32[]{:S(2)}) copy-start(f32[2,512,512]{2,1,0:T(8,128)} %get-tuple-element.184) | copy-start | bytes 6291460 | tf_op jit(solution)/shard_map/while
  492.1 11.0 %collective-permute-start.1 = (f32[2,64,512]{2,1,0:T(8,128)S(1)}, f32[2,64,512]{2,1,0:T(8,128)S(1)}, u32[]{:S(2)}, u32[]{:S(2)}) collective-permute-start(f32[2,64,512]{2,1,0:T(8,128)S(1)} %broadcast_select_fusion.5), channel_id=1, source_target_pairs={{8,0},{16,8},{24,16},{32,24},{40,32},{48,40},{56,48},{64,56},{72,6... | collective-permute-start | bytes 786440 | tf_op jit(solution)/shard_map/while/body/eval_jaxpr/ppermute | solution.py:13
  508.7 9.4 %collective-permute-start.1 = (f32[2,64,512]{2,1,0:T(8,128)S(1)}, f32[2,64,512]{2,1,0:T(8,128)S(1)}, u32[]{:S(2)}, u32[]{:S(2)}) collective-permute-start(f32[2,64,512]{2,1,0:T(8,128)S(1)} %broadcast_select_fusion.5), channel_id=1, source_target_pairs={{8,0},{16,8},{24,16},{32,24},{40,32},{48,40},{56,48},{64,56},{72,6... | collective-permute-start | bytes 786440 | tf_op jit(solution)/shard_map/while/body/eval_jaxpr/ppermute | solution.py:13
  523.7 8.5 %collective-permute-start.1 = (f32[2,64,512]{2,1,0:T(8,128)S(1)}, f32[2,64,512]{2,1,0:T(8,128)S(1)}, u32[]{:S(2)}, u32[]{:S(2)}) collective-permute-start(f32[2,64,512]{2,1,0:T(8,128)S(1)} %broadcast_select_fusion.5), channel_id=1, source_target_pairs={{8,0},{16,8},{24,16},{32,24},{40,32},{48,40},{56,48},{64,56},{72,6... | collective-permute-start | bytes 786440 | tf_op jit(solution)/shard_map/while/body/eval_jaxpr/ppermute | solution.py:13
  537.7 68.6 %copy-start.3 = (f32[2,64,512]{2,1,0:T(8,128)}, f32[2,64,512]{2,1,0:T(8,128)S(1)}, u32[]{:S(2)}) copy-start(f32[2,64,512]{2,1,0:T(8,128)S(1)} %get-tuple-element.47) | copy-start | bytes 786436
  537.7 57.3 %collective-permute-start.2 = (f32[2,64,128]{2,1,0:T(8,128)S(1)}, f32[2,64,128]{2,1,0:T(8,128)S(1)}, u32[]{:S(2)}, u32[]{:S(2)}) collective-permute-start(f32[2,64,128]{2,1,0:T(8,128)S(1)} %get-tuple-element.97), channel_id=1, source_target_pairs={{0,1},{1,2},{2,3},{3,4},{4,5},{5,6},{6,7},{8,9},{9,10},{10,11},{11... | collective-permute-start | bytes 196616 | tf_op jit(solution)/shard_map/ppermute | solution.py:24
  578.2 37.3 %all-to-all-start.2 = ((s32[16,2,1]{1,2,0:T(1,128)}), s32[16,2,1]{1,2,0:T(1,128)S(1)}, u32[]{:S(2)}, u32[]{:S(2)}) async-start(s32[16,2,1]{1,2,0:T(1,128)} %bitcast.15), calls=%async_computation.2 | async-start | bytes 16384 | tf_op jit(solution)/shard_map/all_to_all | solution.py:124
  592.9 5.6 collective-permute-start.3
  615.5 13.1 %all-to-all-start.3 = ((f32[16,2,128]{2,1,0:T(2,128)}), f32[16,2,128]{2,1,0:T(2,128)S(1)}, u32[]{:S(2)}, u32[]{:S(2)}) async-start(f32[16,2,128]{2,1,0:T(2,128)} %bitcast.24), calls=%async_computation.3 | async-start | bytes 32768 | tf_op jit(solution)/shard_map/all_to_all | solution.py:123
  (13 other events, 155.8 us)
where the time goes:
time: 632 us; the launch traced here: 629 us
  waiting for transfers between devices  266 us (42%)
  starting transfers between devices  183 us (29%)
  matrix products  158 us (25%)
  local copies, waits for them, and re-layouts  11.8 us (2%)
  other arithmetic  7.21 us (1%)
    ppermute x32, waiting for transfers between devices, shifted(): return lax.ppermute(block, axis, route)  198 us
    ppermute x32, starting transfers between devices, shifted(): return lax.ppermute(block, axis, route)  105 us
    all_to_all x2, waiting for transfers between devices, body(): lax.all_to_all(outgoing, 'slab', split_axis=0, concat_axis=0, tiled=True)  64.8 us
    dot_general x33, matrix products, complex_product(): jnp.matmul(value_im, panel_re, precision=lax.Precision.HIGHEST)  47.6 us
    dot_general x33, matrix products, complex_product(): jnp.matmul(value_im, panel_im, precision=lax.Precision.HIGHEST)  47.4 us
    ppermute x1, starting transfers between devices, padded(): lax.ppermute(tail, axis, [(i, (i + 1) % count) for i in range(ends)])  39 us
    dot_general x33, matrix products, complex_product(): jnp.matmul(value_re, panel_re, precision=lax.Precision.HIGHEST)  28.2 us
    dot_general x33, matrix products, complex_product(): jnp.matmul(value_re, panel_im, precision=lax.Precision.HIGHEST)  28.2 us
  transfers between devices with their start and end apart: 38, of which 35 were waited for; matrix products, arithmetic and copies ran while one was open for 4% of the time, Pallas kernels for 0%

commit v1 on v0

v1 whole, which is shorter than its diff:
```python
import functools

import jax
import jax.numpy as jnp
from jax import lax
from jax.experimental import pallas as pl
from jax.experimental.pallas import tpu as pltpu
from jax.sharding import PartitionSpec as P

MESH = pl.DeviceIdType.MESH
F32 = jnp.float32
BF16 = jnp.bfloat16
LB = 128
RY = 4
CH = 8


def split(value):
    high = value.astype(BF16)
    low = (value - high.astype(F32)).astype(BF16)
    return high, low


def remote(src, dst, send, recv, axis, where):
    return pltpu.make_async_remote_copy(
        src_ref=src,
        dst_ref=dst,
        send_sem=send,
        recv_sem=recv,
        device_id={axis: where},
        device_id_type=MESH,
    )


def kernel(
    slab_sm,
    pos_sm,
    own_sm,
    slot_sm,
    shot_v,
    wav_v,
    res_hbm,
    down_hbm,
    up_hbm,
    rec_hbm,
    ff_hbm,
    u_out,
    model_out,
    res,
    pan,
    rec,
    ff,
    wd,
    wu,
    wr,
    part,
    h1,
    f1,
    h2,
    f2,
    src,
    dbuf,
    drecv,
    urecv,
    lext,
    rext,
    xr,
    gbuf,
    gsend,
    grecv,
    load_sem,
    h1s,
    h1r,
    f1s,
    f1r,
    h2s,
    h2r,
    f2s,
    f2r,
    ds_,
    dr_,
    us_,
    ur_,
    ls_,
    lr_,
    rs_,
    rr_,
    gs_,
    gr_,
):
    slabs = 16
    lats = 8
    shots, trace = src.shape[1], src.shape[2]
    half = shots // 2
    places = trace // LB
    nres = res.shape[0]
    nch = shots // CH
    me = lax.axis_index("slab")
    lat = lax.axis_index("lat")
    y = lax.rem(me, RY)
    z = lax.div(me, RY)

    loads = [
        pltpu.make_async_copy(res_hbm, res, load_sem.at[0]),
        pltpu.make_async_copy(down_hbm, pan.at[0], load_sem.at[1]),
        pltpu.make_async_copy(up_hbm, pan.at[1], load_sem.at[2]),
        pltpu.make_async_copy(rec_hbm, rec, load_sem.at[3]),
        pltpu.make_async_copy(ff_hbm, ff, load_sem.at[4]),
    ]
    for load in loads:
        load.start()

    barrier = pltpu.get_barrier_semaphore()

    def greet(k, carry):
        other = lax.rem(me + k, slabs)
        pl.semaphore_signal(barrier, inc=1, device_id={"slab": other}, device_id_type=MESH)
        return carry

    lax.fori_loop(1, slabs, greet, 0)

    @pl.when(lat > 0)
    def _():
        pl.semaphore_signal(barrier, inc=1, device_id={"lat": lat - 1}, device_id_type=MESH)

    @pl.when(lat < lats - 1)
    def _():
        pl.semaphore_signal(barrier, inc=1, device_id={"lat": lat + 1}, device_id_type=MESH)

    def ring(col):
        return y if col == 0 else z

    def cross(col):
        return z if col == 0 else y

    def slab_at(col, t, i):
        return i * RY + t if col == 0 else t * RY + i

    def build(col, s):
        rows = pl.ds(half * col, half)

        def add(r, accs):
            block = res[r, :, rows, :]
            tag = slab_sm[r] * places + pos_sm[r]
            return tuple(
                acc + block * jnp.where(tag == s * places + p, 1.0, 0.0).astype(F32)
                for p, acc in enumerate(accs)
            )

        zero = jnp.zeros((2, half, LB), F32)
        accs = lax.fori_loop(0, nres, add, (zero,) * places, unroll=4)
        for p in range(places):
            part[s, :, rows, p * LB : (p + 1) * LB] = accs[p]

    def half_copy(stage, col, i, way, s):
        rows = pl.ds(half * col, half)
        a, b = ring(col), cross(col)
        if stage == 1:
            to = lax.rem(a + (RY - 1 if way == 0 else 1), RY)
            where = slab_at(col, to, b)
            return remote(
                part.at[s, way, rows, :], h1.at[col, i, way], h1s.at[col, i, way], h1r.at[col, i, way], "slab", where
            )
        to = lax.rem(b + (RY - 1 if way == 0 else 1), RY)
        where = slab_at(col, a, to)
        return remote(part.at[s, way, rows, :], h2.at[col, way], h2s.at[col, way], h2r.at[col, way], "slab", where)

    def full_copy(stage, col, i, way, s):
        rows = pl.ds(half * col, half)
        a, b = ring(col), cross(col)
        if stage == 1:
            to = lax.rem(a + (RY - 1 if way == 0 else 1), RY)
            where = slab_at(col, to, b)
            return remote(
                part.at[s, :, rows, :], f1.at[col, i, way], f1s.at[col, i, way], f1r.at[col, i, way], "slab", where
            )
        to = lax.rem(b + (RY - 1 if way == 0 else 1), RY)
        where = slab_at(col, a, to)
        return remote(part.at[s, :, rows, :], f2.at[col, way], f2s.at[col, way], f2r.at[col, way], "slab", where)

    loads[0].wait()

    def first(i, carry):
        for col in (0, 1):
            s = slab_at(col, lax.rem(ring(col) + 2, RY), i)
            build(col, s)
        return carry

    lax.fori_loop(0, RY, first, 0)
    peers = slabs - 1 + (lat > 0).astype(jnp.int32) + (lat < lats - 1).astype(jnp.int32)
    pl.semaphore_wait(barrier, peers)

    def first_send(i, carry):
        for col in (0, 1):
            s = slab_at(col, lax.rem(ring(col) + 2, RY), i)
            for way in (0, 1):
                half_copy(1, col, i, way, s).start()
        return carry

    lax.fori_loop(0, RY, first_send, 0)

    def second(i, carry):
        for col in (0, 1):
            for way in (0, 1):
                t = lax.rem(ring(col) + (RY - 1 if way == 0 else 1), RY)
                s = slab_at(col, t, i)
                rows = pl.ds(half * col, half)
                build(col, s)
                half_copy(1, col, i, way, s).wait_recv()
                part[s, way, rows, :] = part[s, way, rows, :] + h1[col, i, way]
                full_copy(1, col, i, way, s).start()
        return carry

    lax.fori_loop(0, RY, second, 0)

    def own(i, carry):
        for col in (0, 1):
            build(col, slab_at(col, ring(col), i))
        return carry

    lax.fori_loop(0, RY, own, 0)

    def pack(source, which, target, count):
        def col_block(j, carry):
            cols = pl.ds(pl.multiple_of(j * LB, LB), LB)
            for part_no in (0, 1):
                ref = source.at[which] if which is not None else source
                high, low = split(ref[part_no, :, cols])
                target[j, :, part_no * LB : (part_no + 1) * LB] = high
                target[j, :, (2 + part_no) * LB : (3 + part_no) * LB] = low
            return carry

        lax.fori_loop(0, count, col_block, 0)

    loads[1].wait()
    pack(pan, 0, wd, trace // LB)

    def gather(i, carry):
        for col in (0, 1):
            s = slab_at(col, ring(col), i)
            rows = pl.ds(half * col, half)
            for way in (0, 1):
                full_copy(1, col, i, way, s).wait_recv()
            part[s, :, rows, :] = part[s, :, rows, :] + (f1[col, i, 0] + f1[col, i, 1])
        return carry

    lax.fori_loop(0, RY, gather, 0)
    for col in (0, 1):
        i = lax.rem(cross(col) + 2, RY)
        s = slab_at(col, ring(col), i)
        for way in (0, 1):
            half_copy(2, col, i, way, s).start()
    loads[2].wait()
    pack(pan, 1, wu, trace // LB)
    for col in (0, 1):
        rows = pl.ds(half * col, half)
        for way in (0, 1):
            i = lax.rem(cross(col) + (RY - 1 if way == 0 else 1), RY)
            s = slab_at(col, ring(col), i)
            half_copy(2, col, i, way, s).wait_recv()
            part[s, way, rows, :] = part[s, way, rows, :] + h2[col, way]
            full_copy(2, col, i, way, s).start()

    picker = (shot_v[...] == lax.broadcasted_iota(jnp.int32, (shots, shots), 1)).astype(F32)
    weights = jnp.dot(picker, wav_v[...], precision=lax.Precision.HIGHEST, preferred_element_type=F32)

    @pl.when(lat == 0)
    def _():
        lext[...] = jnp.zeros_like(lext)

    @pl.when(lat == lats - 1)
    def _():
        rext[...] = jnp.zeros_like(rext)

    for col in (0, 1):
        rows = pl.ds(half * col, half)
        for way in (0, 1):
            full_copy(2, col, 0, way, me).wait_recv()
        total = part[me, :, rows, :] + (f2[col, 0] + f2[col, 1])
        w_re = weights[half * col : half * (col + 1), 0:1]
        w_im = weights[half * col : half * (col + 1), 1:2]
        src[0, rows, :] = w_re * total[0] - w_im * total[1]
        src[1, rows, :] = w_re * total[1] + w_im * total[0]

    def turn(arrived, target, rows, weight, extra):
        x = jnp.concatenate([arrived[0, rows, :], arrived[1, rows, :]], axis=0)
        high, low = split(x)
        x = jnp.concatenate([high, low], axis=0)
        for j in range(trace // LB):
            cols = slice(j * LB, (j + 1) * LB)
            prod = jnp.dot(x, weight[j], preferred_element_type=F32)
            prod = prod[: 2 * CH] + prod[2 * CH :]
            prod = prod[:, : 2 * LB] + prod[:, 2 * LB :]
            target[0, rows, cols] = prod[:CH, :LB] - prod[CH:, LB:] + extra[0, rows, cols]
            target[1, rows, cols] = prod[:CH, LB:] + prod[CH:, :LB] + extra[1, rows, cols]

    def rows_of(c):
        return pl.ds(pl.multiple_of(c * CH, CH), CH)

    def down_copy(c):
        rows = rows_of(c)
        return remote(
            dbuf.at[:, rows, :], drecv.at[:, rows, :], ds_.at[c], dr_.at[c], "slab", lax.rem(me + 1, slabs)
        )

    def up_copy(c):
        rows = rows_of(c)
        return remote(
            u_out.at[:, rows, :],
            urecv.at[:, rows, :],
            us_.at[c],
            ur_.at[c],
            "slab",
            lax.rem(me + slabs - 1, slabs),
        )

    def right_copy(c):
        rows = rows_of(c)
        return remote(
            u_out.at[:, rows, pl.ds(trace - LB, LB)],
            lext.at[:, rows, :],
            ls_.at[c],
            lr_.at[c],
            "lat",
            lax.rem(lat + 1, lats),
        )

    def left_copy(c):
        rows = rows_of(c)
        return remote(
            u_out.at[:, rows, pl.ds(0, LB)],
            rext.at[:, rows, :],
            rs_.at[c],
            rr_.at[c],
            "lat",
            lax.rem(lat + lats - 1, lats),
        )

    def finish(c):
        @pl.when(me > 0)
        def _():
            up_copy(c).start()

        @pl.when(lat < lats - 1)
        def _():
            right_copy(c).start()

        @pl.when(lat > 0)
        def _():
            left_copy(c).start()

    def down(c, carry):
        rows = rows_of(c)

        @pl.when(me == 0)
        def _():
            dbuf[:, rows, :] = src[:, rows, :]

        @pl.when(me > 0)
        def _():
            down_copy(c).wait_recv()
            turn(drecv, dbuf, rows, wd, src)

        @pl.when(me < slabs - 1)
        def _():
            down_copy(c).start()

        @pl.when(me == slabs - 1)
        def _():
            u_out[:, rows, :] = dbuf[:, rows, :]
            finish(c)

        return carry

    lax.fori_loop(0, nch, down, 0)
    loads[3].wait()
    pack(rec, None, wr, rec.shape[2] // LB)
    loads[4].wait()

    def up(c, carry):
        rows = rows_of(c)
        up_copy(c).wait_recv()
        turn(urecv, u_out, rows, wu, dbuf)
        finish(c)
        return carry

    @pl.when(me < slabs - 1)
    def _():
        lax.fori_loop(0, nch, up, 0)

    def edges(c, carry):
        @pl.when(lat > 0)
        def _():
            right_copy(c).wait_recv()

        @pl.when(lat < lats - 1)
        def _():
            left_copy(c).wait_recv()

        return carry

    def place(value, first_col):
        width = value.shape[-1]
        for part_no in (0, 1):
            high, low = split(value[part_no])
            xr[part_no * shots : (part_no + 1) * shots, first_col : first_col + width] = high
            xr[(2 + part_no) * shots : (3 + part_no) * shots, first_col : first_col + width] = low

    place(u_out[...], LB)
    lax.fori_loop(0, nch, edges, 0)
    place(lext[...], 0)
    place(rext[...], LB + trace)

    def recover(j, carry):
        cols = pl.ds(pl.multiple_of(j * LB, LB), LB)
        prod = jnp.dot(xr[...], wr[j, :, : 2 * LB], preferred_element_type=F32)
        prod = prod[: 2 * shots] + prod[2 * shots :]
        prod = prod + jnp.dot(xr[: 2 * shots, :], wr[j, :, 2 * LB :], preferred_element_type=F32)
        re = prod[:shots, :LB] - prod[shots:, LB:]
        im = prod[:shots, LB:] + prod[shots:, :LB]
        row = jnp.sum(ff[0, :, cols] * re + ff[1, :, cols] * im, axis=0, keepdims=True)
        gbuf[pl.ds(j, 1), :] = row * (shots ** (-0.5))
        return carry

    neb = gbuf.shape[0]
    lax.fori_loop(0, neb, recover, 0)

    grads = gbuf[...]
    lanes = lax.broadcasted_iota(jnp.int32, gsend.shape[1:], 0)
    placed = []
    for b in range(neb):
        row = jnp.broadcast_to(grads[b : b + 1, :], gsend.shape[1:])
        placed.append(jnp.where(lanes == slot_sm[b], row, 0.0))
    for s in range(slabs):
        total = jnp.zeros(gsend.shape[1:], F32)
        for b in range(neb):
            total = total + placed[b] * jnp.where(own_sm[b] == s, 1.0, 0.0).astype(F32)
        gsend[s] = total

    def grad_copy(to, sender):
        return remote(gsend.at[to], grecv.at[sender], gs_.at[to], gr_.at[sender], "slab", to)

    def grad_send(k, carry):
        grad_copy(lax.rem(me + k, slabs), me).start()
        return carry

    lax.fori_loop(1, slabs, grad_send, 0)
    grecv[me] = gsend[me]

    def drain1(i, carry):
        for col in (0, 1):
            s = slab_at(col, lax.rem(ring(col) + 2, RY), i)
            for way in (0, 1):
                half_copy(1, col, i, way, s).wait_send()
                full_copy(1, col, i, way, s).wait_send()
        return carry

    lax.fori_loop(0, RY, drain1, 0)
    for col in (0, 1):
        for way in (0, 1):
            half_copy(2, col, 0, way, me).wait_send()
            full_copy(2, col, 0, way, me).wait_send()

    def drain2(c, carry):
        @pl.when(me < slabs - 1)
        def _():
            down_copy(c).wait_send()

        @pl.when(me > 0)
        def _():
            up_copy(c).wait_send()

        @pl.when(lat < lats - 1)
        def _():
            right_copy(c).wait_send()

        @pl.when(lat > 0)
        def _():
            left_copy(c).wait_send()

        return carry

    lax.fori_loop(0, nch, drain2, 0)

    def grad_wait(k, total):
        other = lax.rem(me + k, slabs)
        grad_copy(other, other).wait_recv()
        return total + grecv[other]

    model_out[...] = lax.fori_loop(1, slabs, grad_wait, grecv[me])

    def grad_drain(k, carry):
        grad_copy(lax.rem(me + k, slabs), me).wait_send()
        return carry

    lax.fori_loop(1, slabs, grad_drain, 0)


def body(
    residual_blocks,
    residual_slab,
    residual_pos,
    shot_ids,
    wavelet,
    down_panel,
    up_panel,
    recovery,
    forward_field,
    element_owner,
    element_slot,
):
    slabs = 16
    nres, _, shots, width = residual_blocks.shape
    trace = down_panel.shape[-1]
    depth, nel = recovery.shape[-2:]
    neb = element_slot.shape[0]
    half = shots // 2
    nch = shots // CH
    smem = pl.BlockSpec(memory_space=pltpu.SMEM)
    vmem = pl.BlockSpec(memory_space=pltpu.VMEM)
    hbm = pl.BlockSpec(memory_space=pl.ANY)
    dma = pltpu.SemaphoreType.DMA
    ups, model = pl.pallas_call(
        kernel,
        out_shape=(
            jax.ShapeDtypeStruct((2, shots, trace), F32),
            jax.ShapeDtypeStruct((neb, width), F32),
        ),
        in_specs=[smem] * 4 + [vmem] * 2 + [hbm] * 5,
        out_specs=(vmem, vmem),
        scratch_shapes=[
            pltpu.VMEM((nres, 2, shots, width), F32),
            pltpu.VMEM((2, 2, trace, trace), F32),
            pltpu.VMEM((2, depth, nel), F32),
            pltpu.VMEM((2, shots, nel), F32),
            pltpu.VMEM((trace // width, trace, 4 * width), BF16),
            pltpu.VMEM((trace // width, trace, 4 * width), BF16),
            pltpu.VMEM((nel // width, depth, 4 * width), BF16),
            pltpu.VMEM((slabs, 2, shots, trace), F32),
            pltpu.VMEM((2, RY, 2, half, trace), F32),
            pltpu.VMEM((2, RY, 2, 2, half, trace), F32),
            pltpu.VMEM((2, 2, half, trace), F32),
            pltpu.VMEM((2, 2, 2, half, trace), F32),
            pltpu.VMEM((2, shots, trace), F32),
            pltpu.VMEM((2, shots, trace), F32),
            pltpu.VMEM((2, shots, trace), F32),
            pltpu.VMEM((2, shots, trace), F32),
            pltpu.VMEM((2, shots, width), F32),
            pltpu.VMEM((2, shots, width), F32),
            pltpu.VMEM((4 * shots, depth), BF16),
            pltpu.VMEM((neb, width), F32),
            pltpu.VMEM((slabs, neb, width), F32),
            pltpu.VMEM((slabs, neb, width), F32),
            dma((5,)),
            dma((2, RY, 2)),
            dma((2, RY, 2)),
            dma((2, RY, 2)),
            dma((2, RY, 2)),
            dma((2, 2)),
            dma((2, 2)),
            dma((2, 2)),
            dma((2, 2)),
            dma((nch,)),
            dma((nch,)),
            dma((nch,)),
            dma((nch,)),
            dma((nch,)),
            dma((nch,)),
            dma((nch,)),
            dma((nch,)),
            dma((slabs,)),
            dma((slabs,)),
        ],
        compiler_params=pltpu.CompilerParams(
            collective_id=0, has_side_effects=True, vmem_limit_bytes=60 * 1024 * 1024
        ),
    )(
        residual_slab.reshape(-1),
        residual_pos,
        element_owner.reshape(-1),
        element_slot,
        shot_ids.reshape(-1, 1),
        wavelet,
        residual_blocks,
        down_panel[0, 0],
        up_panel[0, 0],
        recovery[0, 0],
        forward_field[0, 0],
    )
    return (ups[None, None], model[None, None])


def solution(mesh):
    placed = (
        P(("slab", "lat"), None, None, None),
        P(("slab", "lat"), None),
        P(("slab", "lat")),
        P(),
        P(),
        P("slab", "lat", None, None, None),
        P("slab", "lat", None, None, None),
        P("slab", "lat", None, None, None),
        P("slab", "lat", None, None, None),
        P(("slab", "lat"), None),
        P(("slab", "lat")),
    )
    return jax.shard_map(
        body,
        mesh=mesh,
        in_specs=placed,
        out_specs=(P("slab", "lat", None, None, None), P("slab", "lat", None, None)),
        check_vma=False,
    )
```

time: 632 us -> 165 us (0.26)
  waiting for transfers between devices: 266 us -> 0 us
  starting transfers between devices: 183 us -> 0 us
  matrix products: 158 us -> 0 us
  Pallas kernels: 0 us -> 158 us
  other arithmetic: 7.21 us -> 0 us
    ppermute x34 -> x0, waiting for transfers between devices: 202 us -> none  [the longest x32 198 us: shifted(): return lax.ppermute(block, axis, route)]
    pallas_call x0 -> x1, Pallas kernels: none -> 158 us  [body(): pl.pallas_call(kernel, out_shape=(jax.ShapeDtypeStruct((2, shots, trace),...]
    dot_general x135 -> x0, matrix products: 158 us -> none  [the longest x33 47.6 us: complex_product(): jnp.matmul(value_im, panel_re, precision=lax.Precision.HIGHEST)]
    ppermute x34 -> x0, starting transfers between devices: 147 us -> none  [the longest x32 105 us: shifted(): return lax.ppermute(block, axis, route)]
    all_to_all x4 -> x0, waiting for transfers between devices: 64.8 us -> none  [the longest x2 64.8 us: body(): lax.all_to_all(outgoing, 'slab', split_axis=0, concat_axis=0, tiled=True)]
    all_to_all x4 -> x0, starting transfers between devices: 36.9 us -> none  [the longest x1 14.8 us: body(): lax.all_to_all(outgoing_slot, 'slab', split_axis=0, concat_axis=0, tiled=...]
    scatter x3 -> x0, local copies, waits for them, and re-layouts: 6.91 us -> none  [the longest x1 5.38 us: body(): outgoing = jnp.zeros((slab_count * capacity, 2, shots, width), jnp.float3...]
  transfers between devices with their start and end apart: 38 -> 0, of which waited for: 35 -> 0; matrix products, arithmetic and copies ran while one was open for 4% -> 0% of each run, Pallas kernels for 0% -> 0%
where the time goes in v1:
time: 165 us
  Pallas kernels  158 us (96%)
  local copies, waits for them, and re-layouts  5.67 us (3%)
    pallas_call x1, Pallas kernels, body(): pl.pallas_call(kernel, out_shape=(jax.ShapeDtypeStruct((2, shots, trace),...  158 us
    unnamed x3, local copies, waits for them, and re-layouts  4.31 us

profile of v1, /device:TPU:1, one launch (start us, length us, event | category | flops | bytes accessed | tf_op | source)
XLA Modules:
  0.0 164.5 jit_solution(5198666358872062941)
XLA Ops:
  0.6 1.4 copy.13.shot_v
  2.0 1.4 copy.14.wav_v
  3.4 158.2 %shard_map.122 = (f32[2,64,512]{2,1,0:T(8,128)}, f32[8,128]{1,0:T(8,128)}) custom-call(s32[32]{0:T(128)} %bitcast.16, s32[32]{0:T(128)} %pos_sm.1, s32[8]{0:T(128)} %bitcast.17, s32[8]{0:T(128)} %slot_sm.1, s32[64,1]{1,0:T(8,128)} %copy.13.shot_v, f32[64,2]{1,0:T(8,128)} %copy.14.wav_v, f32[32,2,64,128]{3,2,1,0:T(8,128)} %res_hbm.1, ...), custom_call_target="tpu_custom_call" | custom-call | tf_op jit(solution)/shard_map/pallas_call | solution.py:523
  161.6 1.7 %copy.17 = f32[1,1,2,64,512]{4,3,2,1,0:T(8,128)} copy(f32[1,1,2,64,512]{4,3,2,1,0:T(8,128)} %bitcast.13) | data formatting | bytes 524288
  163.3 1.3 copy.18

commit v2 on v1

--- a/solution.py
+++ b/solution.py
@@ -60,6 +60,7 @@
     f2,
     src,
     dbuf,
+    ubuf,
     drecv,
     urecv,
     lext,
@@ -84,13 +85,20 @@
     ls_,
     lr_,
     rs_,
+    r2s_,
     rr_,
+    as_,
+    ar_,
     gs_,
     gr_,
+    ps_,
+    pr_,
+    ss_,
+    sr_,
 ):
     slabs = 16
     lats = 8
-    shots, trace = src.shape[1], src.shape[2]
+    shots, trace = src.shape[2], src.shape[3]
     half = shots // 2
     places = trace // LB
     nres = res.shape[0]
@@ -100,15 +108,22 @@
     y = lax.rem(me, RY)
     z = lax.div(me, RY)
 
-    loads = [
-        pltpu.make_async_copy(res_hbm, res, load_sem.at[0]),
-        pltpu.make_async_copy(down_hbm, pan.at[0], load_sem.at[1]),
-        pltpu.make_async_copy(up_hbm, pan.at[1], load_sem.at[2]),
-        pltpu.make_async_copy(rec_hbm, rec, load_sem.at[3]),
-        pltpu.make_async_copy(ff_hbm, ff, load_sem.at[4]),
-    ]
-    for load in loads:
-        load.start()
+    core = lax.rem(lat, 2)
+    mate = lat + 1 - 2 * core
+    load_res = pltpu.make_async_copy(res_hbm, res, load_sem.at[0])
+    load_down = pltpu.make_async_copy(down_hbm, pan.at[0], load_sem.at[1])
+    load_up = pltpu.make_async_copy(up_hbm, pan.at[1], load_sem.at[2])
+    load_rec = pltpu.make_async_copy(rec_hbm, rec, load_sem.at[3])
+    load_ff = pltpu.make_async_copy(ff_hbm, ff, load_sem.at[4])
+    load_res.start()
+
+    @pl.when(core == 1)
+    def _():
+        load_down.start()
+        load_up.start()
+
+    load_rec.start()
+    load_ff.start()
 
     barrier = pltpu.get_barrier_semaphore()
 
@@ -119,13 +134,15 @@
 
     lax.fori_loop(1, slabs, greet, 0)
 
-    @pl.when(lat > 0)
-    def _():
-        pl.semaphore_signal(barrier, inc=1, device_id={"lat": lat - 1}, device_id_type=MESH)
-
-    @pl.when(lat < lats - 1)
-    def _():
-        pl.semaphore_signal(barrier, inc=1, device_id={"lat": lat + 1}, device_id_type=MESH)
+    def meet(step, present):
+        @pl.when(present)
+        def _():
+            pl.semaphore_signal(barrier, inc=1, device_id={"lat": lat + step}, device_id_type=MESH)
+
+    meet(-1, lat > 0)
+    meet(1, lat < lats - 1)
+    meet(-2, jnp.logical_and(core == 1, lat > 1))
+    meet(2, jnp.logical_and(core == 1, lat < lats - 1))
 
     def ring(col):
         return y if col == 0 else z
@@ -135,6 +152,10 @@
 
     def slab_at(col, t, i):
         return i * RY + t if col == 0 else t * RY + i
+
+    def order(col, k):
+        off = jnp.where(k < 2, 2 - k, 3 * (3 - k))
+        return lax.rem(cross(col) + off, RY)
 
     def build(col, s):
         rows = pl.ds(half * col, half)
@@ -178,20 +199,31 @@
         where = slab_at(col, a, to)
         return remote(part.at[s, :, rows, :], f2.at[col, way], f2s.at[col, way], f2r.at[col, way], "slab", where)
 
-    loads[0].wait()
-
-    def first(i, carry):
+    load_res.wait()
+
+    def first(k, carry):
         for col in (0, 1):
+            i = order(col, k)
             s = slab_at(col, lax.rem(ring(col) + 2, RY), i)
             build(col, s)
         return carry
 
     lax.fori_loop(0, RY, first, 0)
     peers = slabs - 1 + (lat > 0).astype(jnp.int32) + (lat < lats - 1).astype(jnp.int32)
+    peers = peers + core * ((lat > 1).astype(jnp.int32) + (lat < lats - 1).astype(jnp.int32))
     pl.semaphore_wait(barrier, peers)
 
-    def first_send(i, carry):
+    def panel_copy(which):
+        ref = down_hbm if which == 0 else up_hbm
+        return remote(ref, pan.at[2 + which], ps_.at[which], pr_.at[which], "lat", mate)
+
+    @pl.when(core == 0)
+    def _():
+        panel_copy(0).start()
+
+    def first_send(k, carry):
         for col in (0, 1):
+            i = order(col, k)
             s = slab_at(col, lax.rem(ring(col) + 2, RY), i)
             for way in (0, 1):
                 half_copy(1, col, i, way, s).start()
@@ -199,8 +231,9 @@
 
     lax.fori_loop(0, RY, first_send, 0)
 
-    def second(i, carry):
+    def second(k, carry):
         for col in (0, 1):
+            i = order(col, k)
             for way in (0, 1):
                 t = lax.rem(ring(col) + (RY - 1 if way == 0 else 1), RY)
                 s = slab_at(col, t, i)
@@ -232,11 +265,19 @@
 
         lax.fori_loop(0, count, col_block, 0)
 
-    loads[1].wait()
-    pack(pan, 0, wd, trace // LB)
-
-    def gather(i, carry):
+    @pl.when(core == 1)
+    def _():
+        load_down.wait()
+        pack(pan, 0, wd.at[1], trace // LB)
+
+    @pl.when(core == 0)
+    def _():
+        panel_copy(1).start()
+
+
+    def gather(k, carry):
         for col in (0, 1):
+            i = order(col, k)
             s = slab_at(col, ring(col), i)
             rows = pl.ds(half * col, half)
             for way in (0, 1):
@@ -244,14 +285,13 @@
             part[s, :, rows, :] = part[s, :, rows, :] + (f1[col, i, 0] + f1[col, i, 1])
         return carry
 
-    lax.fori_loop(0, RY, gather, 0)
+    lax.fori_loop(0, 1, gather, 0)
     for col in (0, 1):
         i = lax.rem(cross(col) + 2, RY)
         s = slab_at(col, ring(col), i)
         for way in (0, 1):
             half_copy(2, col, i, way, s).start()
-    loads[2].wait()
-    pack(pan, 1, wu, trace // LB)
+    lax.fori_loop(1, RY, gather, 0)
     for col in (0, 1):
         rows = pl.ds(half * col, half)
         for way in (0, 1):
@@ -261,6 +301,18 @@
             part[s, way, rows, :] = part[s, way, rows, :] + h2[col, way]
             full_copy(2, col, i, way, s).start()
 
+    @pl.when(core == 1)
+    def _():
+        panel_copy(0).wait_recv()
+        pack(pan, 2, wd.at[0], trace // LB)
+        load_up.wait()
+        pack(pan, 1, wu.at[1], trace // LB)
+
+    @pl.when(core == 0)
+    def _():
+        load_rec.wait()
+        pack(rec, None, wr, rec.shape[2] // LB)
+
     picker = (shot_v[...] == lax.broadcasted_iota(jnp.int32, (shots, shots), 1)).astype(F32)
     weights = jnp.dot(picker, wav_v[...], precision=lax.Precision.HIGHEST, preferred_element_type=F32)
 
@@ -271,6 +323,10 @@
     @pl.when(lat == lats - 1)
     def _():
         rext[...] = jnp.zeros_like(rext)
+
+    def source_copy(col):
+        rows = pl.ds(half * col, half)
+        return remote(src.at[0, :, rows, :], src.at[0, :, rows, :], ss_.at[col], sr_.at[col], "lat", mate)
 
     for col in (0, 1):
         rows = pl.ds(half * col, half)
@@ -279,8 +335,12 @@
         total = part[me, :, rows, :] + (f2[col, 0] + f2[col, 1])
         w_re = weights[half * col : half * (col + 1), 0:1]
         w_im = weights[half * col : half * (col + 1), 1:2]
-        src[0, rows, :] = w_re * total[0] - w_im * total[1]
-        src[1, rows, :] = w_re * total[1] + w_im * total[0]
+        src[core, 0, rows, :] = w_re * total[0] - w_im * total[1]
+        src[core, 1, rows, :] = w_re * total[1] + w_im * total[0]
+
+        @pl.when(core == 0)
+        def _():
+            source_copy(col).start()
 
     def turn(arrived, target, rows, weight, extra):
         x = jnp.concatenate([arrived[0, rows, :], arrived[1, rows, :]], axis=0)
@@ -297,105 +357,141 @@
     def rows_of(c):
         return pl.ds(pl.multiple_of(c * CH, CH), CH)
 
-    def down_copy(c):
+    def down_copy(c, w):
         rows = rows_of(c)
         return remote(
-            dbuf.at[:, rows, :], drecv.at[:, rows, :], ds_.at[c], dr_.at[c], "slab", lax.rem(me + 1, slabs)
+            dbuf.at[w, :, rows, :],
+            drecv.at[w, :, rows, :],
+            ds_.at[w, c],
+            dr_.at[w, c],
+            "slab",
+            lax.rem(me + 1, slabs),
         )
 
-    def up_copy(c):
+    def up_copy(c, w):
         rows = rows_of(c)
         return remote(
-            u_out.at[:, rows, :],
-            urecv.at[:, rows, :],
-            us_.at[c],
-            ur_.at[c],
+            ubuf.at[w, :, rows, :],
+            urecv.at[w, :, rows, :],
+            us_.at[w, c],
+            ur_.at[w, c],
             "slab",
             lax.rem(me + slabs - 1, slabs),
         )
 
-    def right_copy(c):
+    def last_cells(c, w, to):
         rows = rows_of(c)
         return remote(
-            u_out.at[:, rows, pl.ds(trace - LB, LB)],
-            lext.at[:, rows, :],
-            ls_.at[c],
-            lr_.at[c],
-            "lat",
-            lax.rem(lat + 1, lats),
+            ubuf.at[w, :, rows, pl.ds(trace - LB, LB)], lext.at[:, rows, :], ls_.at[c], lr_.at[c], "lat", to
         )
 
-    def left_copy(c):
+    def first_cells(c, w, to):
         rows = rows_of(c)
-        return remote(
-            u_out.at[:, rows, pl.ds(0, LB)],
-            rext.at[:, rows, :],
-            rs_.at[c],
-            rr_.at[c],
-            "lat",
-            lax.rem(lat + lats - 1, lats),
-        )
-
-    def finish(c):
+        send = rs_ if w == 1 else r2s_
+        return remote(ubuf.at[w, :, rows, pl.ds(0, LB)], rext.at[:, rows, :], send.at[c], rr_.at[c], "lat", to)
+
+    def back_copy(c):
+        rows = rows_of(c)
+        return remote(ubuf.at[0, :, rows, :], u_out.at[:, rows, :], as_.at[c], ar_.at[c], "lat", mate)
+
+    after = lax.rem(lat + 1, lats)
+    before2 = lax.rem(lat + lats - 2, lats)
+
+    def finish(c, w):
+        rows = rows_of(c)
+
         @pl.when(me > 0)
         def _():
-            up_copy(c).start()
-
-        @pl.when(lat < lats - 1)
-        def _():
-            right_copy(c).start()
-
-        @pl.when(lat > 0)
-        def _():
-            left_copy(c).start()
+            up_copy(c, w).start()
+
+        if w == 0:
+            back_copy(c).start()
+
+            @pl.when(lat > 1)
+            def _():
+                first_cells(c, 0, before2).start()
+
+            lext[:, rows, :] = ubuf[0, :, rows, trace - LB :]
+        else:
+            first_cells(c, 1, mate).start()
+
+            @pl.when(lat < lats - 1)
+            def _():
+                last_cells(c, 1, after).start()
+
+            u_out[:, rows, :] = ubuf[1, :, rows, :]
 
     def down(c, carry):
         rows = rows_of(c)
-
-        @pl.when(me == 0)
-        def _():
-            dbuf[:, rows, :] = src[:, rows, :]
-
-        @pl.when(me > 0)
-        def _():
-            down_copy(c).wait_recv()
-            turn(drecv, dbuf, rows, wd, src)
-
-        @pl.when(me < slabs - 1)
-        def _():
-            down_copy(c).start()
-
-        @pl.when(me == slabs - 1)
-        def _():
-            u_out[:, rows, :] = dbuf[:, rows, :]
-            finish(c)
-
-        return carry
-
-    lax.fori_loop(0, nch, down, 0)
-    loads[3].wait()
-    pack(rec, None, wr, rec.shape[2] // LB)
-    loads[4].wait()
+        for w in (1, 0):
+
+            @pl.when(me == 0)
+            def _():
+                dbuf[w, :, rows, :] = src[w, :, rows, :]
+
+            @pl.when(me > 0)
+            def _():
+                down_copy(c, w).wait_recv()
+                turn(drecv.at[w], dbuf.at[w], rows, wd.at[w], src.at[w])
+
+            @pl.when(me < slabs - 1)
+            def _():
+                down_copy(c, w).start()
+
+            @pl.when(me == slabs - 1)
+            def _():
+                ubuf[w, :, rows, :] = dbuf[w, :, rows, :]
+                finish(c, w)
+
+        return carry
 
     def up(c, carry):
         rows = rows_of(c)
-        up_copy(c).wait_recv()
-        turn(urecv, u_out, rows, wu, dbuf)
-        finish(c)
-        return carry
-
-    @pl.when(me < slabs - 1)
-    def _():
-        lax.fori_loop(0, nch, up, 0)
+        for w in (1, 0):
+            up_copy(c, w).wait_recv()
+            turn(urecv.at[w], ubuf.at[w], rows, wu.at[w], dbuf.at[w])
+            finish(c, w)
+        return carry
+
+    def late_packs():
+        panel_copy(1).wait_recv()
+        pack(pan, 3, wu.at[0], trace // LB)
+        load_rec.wait()
+        pack(rec, None, wr, rec.shape[2] // LB)
+
+    @pl.when(core == 1)
+    def _():
+        @pl.when(me >= slabs // 2)
+        def _():
+            late_packs()
+
+        for col in (0, 1):
+            source_copy(col).wait_recv()
+        lax.fori_loop(0, nch, down, 0)
+
+        @pl.when(me < slabs // 2)
+        def _():
+            late_packs()
+
+        @pl.when(me < slabs - 1)
+        def _():
+            lax.fori_loop(0, nch, up, 0)
+
+    load_ff.wait()
 
     def edges(c, carry):
-        @pl.when(lat > 0)
-        def _():
-            right_copy(c).wait_recv()
-
-        @pl.when(lat < lats - 1)
-        def _():
-            left_copy(c).wait_recv()
+        @pl.when(core == 0)
+        def _():
+            back_copy(c).wait_recv()
+            first_cells(c, 1, mate).wait_recv()
+
+        @pl.when(jnp.logical_and(core == 0, lat > 0))
+        def _():
+            last_cells(c, 1, after).wait_recv()
+
+        @pl.when(jnp.logical_and(core == 1, lat < lats - 1))
+        def _():
+            first_cells(c, 0, before2).wait_recv()
 
         return carry
 
@@ -406,8 +502,8 @@
             xr[part_no * shots : (part_no + 1) * shots, first_col : first_col + width] = high
             xr[(2 + part_no) * shots : (3 + part_no) * shots, first_col : first_col + width] = low
 
+    lax.fori_loop(0, nch, edges, 0)
     place(u_out[...], LB)
-    lax.fori_loop(0, nch, edges, 0)
     place(lext[...], 0)
     place(rext[...], LB + trace)
 
@@ -462,25 +558,38 @@
             full_copy(2, col, 0, way, me).wait_send()
 
     def drain2(c, carry):
-        @pl.when(me < slabs - 1)
-        def _():
-            down_copy(c).wait_send()
-
-        @pl.when(me > 0)
-        def _():
-            up_copy(c).wait_send()
+        for w in (0, 1):
+
+            @pl.when(me < slabs - 1)
+            def _():
+                down_copy(c, w).wait_send()
+
+            @pl.when(me > 0)
+            def _():
+                up_copy(c, w).wait_send()
+
+        back_copy(c).wait_send()
+        first_cells(c, 1, mate).wait_send()
+
+        @pl.when(lat > 1)
+        def _():
+            first_cells(c, 0, before2).wait_send()
 
         @pl.when(lat < lats - 1)
         def _():
-            right_copy(c).wait_send()
-
-        @pl.when(lat > 0)
-        def _():
-            left_copy(c).wait_send()
-
-        return carry
-
-    lax.fori_loop(0, nch, drain2, 0)
+            last_cells(c, 1, after).wait_send()
+
+        return carry
+
+    @pl.when(core == 1)
+    def _():
+        lax.fori_loop(0, nch, drain2, 0)
+
+    @pl.when(core == 0)
+    def _():
+        for k in (0, 1):
+            panel_copy(k).wait_send()
+            source_copy(k).wait_send()
 
     def grad_wait(k, total):
         other = lax.rem(me + k, slabs)
@@ -530,21 +639,22 @@
         out_specs=(vmem, vmem),
         scratch_shapes=[
             pltpu.VMEM((nres, 2, shots, width), F32),
-            pltpu.VMEM((2, 2, trace, trace), F32),
+            pltpu.VMEM((4, 2, trace, trace), F32),
             pltpu.VMEM((2, depth, nel), F32),
             pltpu.VMEM((2, shots, nel), F32),
-            pltpu.VMEM((trace // width, trace, 4 * width), BF16),
-            pltpu.VMEM((trace // width, trace, 4 * width), BF16),
+            pltpu.VMEM((2, trace // width, trace, 4 * width), BF16),
+            pltpu.VMEM((2, trace // width, trace, 4 * width), BF16),
             pltpu.VMEM((nel // width, depth, 4 * width), BF16),
             pltpu.VMEM((slabs, 2, shots, trace), F32),
             pltpu.VMEM((2, RY, 2, half, trace), F32),
             pltpu.VMEM((2, RY, 2, 2, half, trace), F32),
             pltpu.VMEM((2, 2, half, trace), F32),
             pltpu.VMEM((2, 2, 2, half, trace), F32),
-            pltpu.VMEM((2, shots, trace), F32),
-            pltpu.VMEM((2, shots, trace), F32),
-            pltpu.VMEM((2, shots, trace), F32),
-            pltpu.VMEM((2, shots, trace), F32),
+            pltpu.VMEM((2, 2, shots, trace), F32),
+            pltpu.VMEM((2, 2, shots, trace), F32),
+            pltpu.VMEM((2, 2, shots, trace), F32),
+            pltpu.VMEM((2, 2, shots, trace), F32),
+            pltpu.VMEM((2, 2, shots, trace), F32),
             pltpu.VMEM((2, shots, width), F32),
             pltpu.VMEM((2, shots, width), F32),
             pltpu.VMEM((4 * shots, depth), BF16),
@@ -560,7 +670,10 @@
             dma((2, 2)),
             dma((2, 2)),
             dma((2, 2)),
-            dma((nch,)),
+            dma((2, nch)),
+            dma((2, nch)),
+            dma((2, nch)),
+            dma((2, nch)),
             dma((nch,)),
             dma((nch,)),
             dma((nch,)),
@@ -570,6 +683,10 @@
             dma((nch,)),
             dma((slabs,)),
             dma((slabs,)),
+            dma((2,)),
+            dma((2,)),
+            dma((2,)),
+            dma((2,)),
         ],
         compiler_params=pltpu.CompilerParams(
             collective_id=0, has_side_effects=True, vmem_limit_bytes=60 * 1024 * 1024

time: 165 us -> 145 us (0.88)
  Pallas kernels: 158 us -> 139 us
    pallas_call x1, Pallas kernels: 158 us -> 139 us  [body(): pl.pallas_call(kernel, out_shape=(jax.ShapeDtypeStruct((2, shots, trace),...]
where the time goes in v2:
time: 145 us
  Pallas kernels  139 us (96%)
  local copies, waits for them, and re-layouts  5.67 us (4%)
    pallas_call x1, Pallas kernels, body(): pl.pallas_call(kernel, out_shape=(jax.ShapeDtypeStruct((2, shots, trace),...  139 us
    unnamed x3, local copies, waits for them, and re-layouts  4.31 us

profile of v2, /device:TPU:1, one launch (start us, length us, event | category | flops | bytes accessed | tf_op | source)
XLA Modules:
  0.0 145.2 jit_solution(12835947764112922272)
XLA Ops:
  0.6 1.4 copy.13.shot_v
  2.0 1.4 copy.14.wav_v
  3.4 138.9 %shard_map.122 = (f32[2,64,512]{2,1,0:T(8,128)}, f32[8,128]{1,0:T(8,128)}) custom-call(s32[32]{0:T(128)} %bitcast.16, s32[32]{0:T(128)} %pos_sm.1, s32[8]{0:T(128)} %bitcast.17, s32[8]{0:T(128)} %slot_sm.1, s32[64,1]{1,0:T(8,128)} %copy.13.shot_v, f32[64,2]{1,0:T(8,128)} %copy.14.wav_v, f32[32,2,64,128]{3,2,1,0:T(8,128)} %res_hbm.1, ...), custom_call_target="tpu_custom_call" | custom-call | tf_op jit(solution)/shard_map/pallas_call | solution.py:632
  142.2 1.7 %copy.17 = f32[1,1,2,64,512]{4,3,2,1,0:T(8,128)} copy(f32[1,1,2,64,512]{4,3,2,1,0:T(8,128)} %bitcast.13) | data formatting | bytes 524288
  143.9 1.3 copy.18

commit v3 on v2

--- a/solution.py
+++ b/solution.py
@@ -12,7 +12,9 @@
 BF16 = jnp.bfloat16
 LB = 128
 RY = 4
+CAP = 4
 CH = 8
+NS = 1
 
 
 def split(value):
@@ -33,18 +35,18 @@
 
 
 def kernel(
-    slab_sm,
-    pos_sm,
+    slab_v,
+    pos_v,
     own_sm,
     slot_sm,
-    shot_v,
-    wav_v,
+    shot_sm,
+    wav_sm,
     res_hbm,
     down_hbm,
     up_hbm,
     rec_hbm,
     ff_hbm,
-    u_out,
+    u_hbm,
     model_out,
     res,
     pan,
@@ -69,6 +71,9 @@
     gbuf,
     gsend,
     grecv,
+    tab_v,
+    tab_sm,
+    wbuf,
     load_sem,
     h1s,
     h1r,
@@ -127,12 +132,9 @@
 
     barrier = pltpu.get_barrier_semaphore()
 
-    def greet(k, carry):
-        other = lax.rem(me + k, slabs)
-        pl.semaphore_signal(barrier, inc=1, device_id={"slab": other}, device_id_type=MESH)
-        return carry
-
-    lax.fori_loop(1, slabs, greet, 0)
+    for step in (1, RY - 1):
+        for other in (z * RY + lax.rem(y + step, RY), lax.rem(z + step, RY) * RY + y):
+            pl.semaphore_signal(barrier, inc=1, device_id={"slab": other}, device_id_type=MESH)
 
     def meet(step, present):
         @pl.when(present)
@@ -144,6 +146,31 @@
     meet(-2, jnp.logical_and(core == 1, lat > 1))
     meet(2, jnp.logical_and(core == 1, lat < lats - 1))
 
+    rows_no = lax.broadcasted_iota(jnp.int32, (1, nres), 1)
+    match = slab_v[...] == lax.broadcasted_iota(jnp.int32, (slabs, nres), 0)
+    hits = jnp.where(match, 1.0, 0.0).astype(F32)
+    before = lax.broadcasted_iota(jnp.int32, (nres, nres), 0) < lax.broadcasted_iota(jnp.int32, (nres, nres), 1)
+    rank = jnp.dot(hits.astype(BF16), jnp.where(before, 1.0, 0.0).astype(BF16), preferred_element_type=F32)
+    code = (rows_no * 8 + pos_v[...]).astype(F32)
+    found = jnp.sum(hits, axis=1, keepdims=True)
+    lane = lax.broadcasted_iota(jnp.int32, tab_v.shape, 1)
+    table = jnp.zeros(tab_v.shape, F32)
+    for c in range(CAP):
+        value = jnp.sum(jnp.where(rank == c, hits * code, 0.0), axis=1, keepdims=True)
+        value = jnp.where(found > c, value, 7.0)
+        table = table + jnp.where(lane == c, value, 0.0)
+    tab_v[...] = table.astype(jnp.int32)
+    load_tab = pltpu.make_async_copy(tab_v, tab_sm, load_sem.at[5])
+    load_tab.start()
+
+    def weight_row(j, carry):
+        for part_no in (0, 1):
+            wbuf[part_no, pl.ds(j, 1), :] = jnp.full((1, LB), wav_sm[part_no, shot_sm[j]], F32)
+        return carry
+
+    lax.fori_loop(0, shots, weight_row, 0, unroll=8)
+    load_tab.wait()
+
     def ring(col):
         return y if col == 0 else z
 
@@ -159,19 +186,14 @@
 
     def build(col, s):
         rows = pl.ds(half * col, half)
-
-        def add(r, accs):
-            block = res[r, :, rows, :]
-            tag = slab_sm[r] * places + pos_sm[r]
-            return tuple(
-                acc + block * jnp.where(tag == s * places + p, 1.0, 0.0).astype(F32)
-                for p, acc in enumerate(accs)
-            )
-
-        zero = jnp.zeros((2, half, LB), F32)
-        accs = lax.fori_loop(0, nres, add, (zero,) * places, unroll=4)
+        codes = [tab_sm[s, c] for c in range(CAP)]
+        blocks = [res[lax.bitwise_and(lax.shift_right_logical(code, 3), nres - 1), :, rows, :] for code in codes]
+        spots = [lax.bitwise_and(code, 7) for code in codes]
         for p in range(places):
-            part[s, :, rows, p * LB : (p + 1) * LB] = accs[p]
+            total = blocks[0] * jnp.where(spots[0] == p, 1.0, 0.0).astype(F32)
+            for c in range(1, CAP):
+                total = total + blocks[c] * jnp.where(spots[c] == p, 1.0, 0.0).astype(F32)
+            part[s, :, rows, p * LB : (p + 1) * LB] = total
 
     def half_copy(stage, col, i, way, s):
         rows = pl.ds(half * col, half)
@@ -180,11 +202,11 @@
             to = lax.rem(a + (RY - 1 if way == 0 else 1), RY)
             where = slab_at(col, to, b)
             return remote(
-                part.at[s, way, rows, :], h1.at[col, i, way], h1s.at[col, i, way], h1r.at[col, i, way], "slab", where
+                part.at[s, way, rows, :], h1.at[col, i, way], h1s, h1r.at[col, i, way], "slab", where
             )
         to = lax.rem(b + (RY - 1 if way == 0 else 1), RY)
         where = slab_at(col, a, to)
-        return remote(part.at[s, way, rows, :], h2.at[col, way], h2s.at[col, way], h2r.at[col, way], "slab", where)
+        return remote(part.at[s, way, rows, :], h2.at[col, way], h2s, h2r.at[col, way], "slab", where)
 
     def full_copy(stage, col, i, way, s):
         rows = pl.ds(half * col, half)
@@ -193,11 +215,11 @@
             to = lax.rem(a + (RY - 1 if way == 0 else 1), RY)
             where = slab_at(col, to, b)
             return remote(
-                part.at[s, :, rows, :], f1.at[col, i, way], f1s.at[col, i, way], f1r.at[col, i, way], "slab", where
+                part.at[s, :, rows, :], f1.at[col, i, way], f1s, f1r.at[col, i, way], "slab", where
             )
         to = lax.rem(b + (RY - 1 if way == 0 else 1), RY)
         where = slab_at(col, a, to)
-        return remote(part.at[s, :, rows, :], f2.at[col, way], f2s.at[col, way], f2r.at[col, way], "slab", where)
+        return remote(part.at[s, :, rows, :], f2.at[col, way], f2s, f2r.at[col, way], "slab", where)
 
     load_res.wait()
 
@@ -209,7 +231,7 @@
         return carry
 
     lax.fori_loop(0, RY, first, 0)
-    peers = slabs - 1 + (lat > 0).astype(jnp.int32) + (lat < lats - 1).astype(jnp.int32)
+    peers = 4 + (lat > 0).astype(jnp.int32) + (lat < lats - 1).astype(jnp.int32)
     peers = peers + core * ((lat > 1).astype(jnp.int32) + (lat < lats - 1).astype(jnp.int32))
     pl.semaphore_wait(barrier, peers)
 
@@ -313,9 +335,6 @@
         load_rec.wait()
         pack(rec, None, wr, rec.shape[2] // LB)
 
-    picker = (shot_v[...] == lax.broadcasted_iota(jnp.int32, (shots, shots), 1)).astype(F32)
-    weights = jnp.dot(picker, wav_v[...], precision=lax.Precision.HIGHEST, preferred_element_type=F32)
-
     @pl.when(lat == 0)
     def _():
         lext[...] = jnp.zeros_like(lext)
@@ -333,8 +352,8 @@
         for way in (0, 1):
             full_copy(2, col, 0, way, me).wait_recv()
         total = part[me, :, rows, :] + (f2[col, 0] + f2[col, 1])
-        w_re = weights[half * col : half * (col + 1), 0:1]
-        w_im = weights[half * col : half * (col + 1), 1:2]
+        w_re = jnp.tile(wbuf[0, rows, :], (1, places))
+        w_im = jnp.tile(wbuf[1, rows, :], (1, places))
         src[core, 0, rows, :] = w_re * total[0] - w_im * total[1]
         src[core, 1, rows, :] = w_re * total[1] + w_im * total[0]
 
@@ -342,84 +361,85 @@
         def _():
             source_copy(col).start()
 
-    def turn(arrived, target, rows, weight, extra):
+    def turn(arrived, target, rows, weight, extra, piece):
         x = jnp.concatenate([arrived[0, rows, :], arrived[1, rows, :]], axis=0)
         high, low = split(x)
         x = jnp.concatenate([high, low], axis=0)
-        for j in range(trace // LB):
-            cols = slice(j * LB, (j + 1) * LB)
-            prod = jnp.dot(x, weight[j], preferred_element_type=F32)
-            prod = prod[: 2 * CH] + prod[2 * CH :]
-            prod = prod[:, : 2 * LB] + prod[:, 2 * LB :]
-            target[0, rows, cols] = prod[:CH, :LB] - prod[CH:, LB:] + extra[0, rows, cols]
-            target[1, rows, cols] = prod[:CH, LB:] + prod[CH:, :LB] + extra[1, rows, cols]
+        count = trace // LB
+        group = count // NS
+        prods = [jnp.dot(x, weight[j], preferred_element_type=F32) for j in range(min(group + 1, count))]
+        for k in range(NS):
+            for j in range(k * group, (k + 1) * group):
+                cols = slice(j * LB, (j + 1) * LB)
+                prod = prods[j][: 2 * CH] + prods[j][2 * CH :]
+                prod = prod[:, : 2 * LB] + prod[:, 2 * LB :]
+                target[0, rows, cols] = prod[:CH, :LB] - prod[CH:, LB:] + extra[0, rows, cols]
+                target[1, rows, cols] = prod[:CH, LB:] + prod[CH:, :LB] + extra[1, rows, cols]
+            piece(k).start()
+            for j in range(len(prods), min(len(prods) + group, count)):
+                prods.append(jnp.dot(x, weight[j], preferred_element_type=F32))
 
     def rows_of(c):
         return pl.ds(pl.multiple_of(c * CH, CH), CH)
 
-    def down_copy(c, w):
-        rows = rows_of(c)
+    def cols_of(k):
+        return pl.ds(0, trace) if k is None else pl.ds(k * (trace // NS), trace // NS)
+
+    def down_copy(c, w, k=None):
+        rows, cols = rows_of(c), cols_of(k)
         return remote(
-            dbuf.at[w, :, rows, :],
-            drecv.at[w, :, rows, :],
-            ds_.at[w, c],
+            dbuf.at[w, :, rows, cols],
+            drecv.at[w, :, rows, cols],
+            ds_,
             dr_.at[w, c],
             "slab",
             lax.rem(me + 1, slabs),
         )
 
-    def up_copy(c, w):
-        rows = rows_of(c)
+    def up_copy(c, w, k=None):
+        rows, cols = rows_of(c), cols_of(k)
         return remote(
-            ubuf.at[w, :, rows, :],
-            urecv.at[w, :, rows, :],
-            us_.at[w, c],
+            ubuf.at[w, :, rows, cols],
+            urecv.at[w, :, rows, cols],
+            us_,
             ur_.at[w, c],
             "slab",
             lax.rem(me + slabs - 1, slabs),
         )
 
-    def last_cells(c, w, to):
-        rows = rows_of(c)
+    def last_cells(rows, w, h, to):
         return remote(
-            ubuf.at[w, :, rows, pl.ds(trace - LB, LB)], lext.at[:, rows, :], ls_.at[c], lr_.at[c], "lat", to
+            ubuf.at[w, :, rows, pl.ds(trace - LB, LB)], lext.at[:, rows, :], ls_, lr_.at[h], "lat", to
         )
 
-    def first_cells(c, w, to):
-        rows = rows_of(c)
+    def first_cells(rows, w, h, to):
         send = rs_ if w == 1 else r2s_
-        return remote(ubuf.at[w, :, rows, pl.ds(0, LB)], rext.at[:, rows, :], send.at[c], rr_.at[c], "lat", to)
-
-    def back_copy(c):
-        rows = rows_of(c)
-        return remote(ubuf.at[0, :, rows, :], u_out.at[:, rows, :], as_.at[c], ar_.at[c], "lat", mate)
+        return remote(ubuf.at[w, :, rows, pl.ds(0, LB)], rext.at[:, rows, :], send, rr_.at[h], "lat", to)
+
+    def back_copy(rows, h):
+        return remote(ubuf.at[0, :, rows, :], ubuf.at[0, :, rows, :], as_, ar_.at[h], "lat", mate)
 
     after = lax.rem(lat + 1, lats)
     before2 = lax.rem(lat + lats - 2, lats)
 
     def finish(c, w):
         rows = rows_of(c)
-
-        @pl.when(me > 0)
-        def _():
-            up_copy(c, w).start()
+        h = lax.div(c, nch // 2)
 
         if w == 0:
-            back_copy(c).start()
+            back_copy(rows, h).start()
 
             @pl.when(lat > 1)
             def _():
-                first_cells(c, 0, before2).start()
+                first_cells(rows, 0, h, before2).start()
 
             lext[:, rows, :] = ubuf[0, :, rows, trace - LB :]
         else:
-            first_cells(c, 1, mate).start()
+            first_cells(rows, 1, h, mate).start()
 
             @pl.when(lat < lats - 1)
             def _():
-                last_cells(c, 1, after).start()
-
-            u_out[:, rows, :] = ubuf[1, :, rows, :]
+                last_cells(rows, 1, h, after).start()
 
     def down(c, carry):
         rows = rows_of(c)
@@ -428,19 +448,17 @@
             @pl.when(me == 0)
             def _():
                 dbuf[w, :, rows, :] = src[w, :, rows, :]
+                down_copy(c, w).start()
 
             @pl.when(me > 0)
             def _():
                 down_copy(c, w).wait_recv()
-                turn(drecv.at[w], dbuf.at[w], rows, wd.at[w], src.at[w])
-
-            @pl.when(me < slabs - 1)
-            def _():
-                down_copy(c, w).start()
+                turn(drecv.at[w], dbuf.at[w], rows, wd.at[w], src.at[w], lambda k: down_copy(c, w, k))
 
             @pl.when(me == slabs - 1)
             def _():
                 ubuf[w, :, rows, :] = dbuf[w, :, rows, :]
+                up_copy(c, w).start()
                 finish(c, w)
 
         return carry
@@ -449,7 +467,7 @@
         rows = rows_of(c)
         for w in (1, 0):
             up_copy(c, w).wait_recv()
-            turn(urecv.at[w], ubuf.at[w], rows, wu.at[w], dbuf.at[w])
+            turn(urecv.at[w], ubuf.at[w], rows, wu.at[w], dbuf.at[w], lambda k: up_copy(c, w, k))
             finish(c, w)
         return carry
 
@@ -479,49 +497,61 @@
 
     load_ff.wait()
 
-    def edges(c, carry):
+    def arrive(h):
+        rows = pl.ds(half * h, half)
+
         @pl.when(core == 0)
         def _():
-            back_copy(c).wait_recv()
-            first_cells(c, 1, mate).wait_recv()
+            back_copy(rows, h).wait_recv()
+            first_cells(rows, 1, h, mate).wait_recv()
 
         @pl.when(jnp.logical_and(core == 0, lat > 0))
         def _():
-            last_cells(c, 1, after).wait_recv()
+            last_cells(rows, 1, h, after).wait_recv()
 
         @pl.when(jnp.logical_and(core == 1, lat < lats - 1))
         def _():
-            first_cells(c, 0, before2).wait_recv()
-
-        return carry
-
-    def place(value, first_col):
+            first_cells(rows, 0, h, before2).wait_recv()
+
+    def place(h, value, first_col):
         width = value.shape[-1]
         for part_no in (0, 1):
             high, low = split(value[part_no])
-            xr[part_no * shots : (part_no + 1) * shots, first_col : first_col + width] = high
-            xr[(2 + part_no) * shots : (3 + part_no) * shots, first_col : first_col + width] = low
-
-    lax.fori_loop(0, nch, edges, 0)
-    place(u_out[...], LB)
-    place(lext[...], 0)
-    place(rext[...], LB + trace)
-
-    def recover(j, carry):
-        cols = pl.ds(pl.multiple_of(j * LB, LB), LB)
-        prod = jnp.dot(xr[...], wr[j, :, : 2 * LB], preferred_element_type=F32)
-        prod = prod[: 2 * shots] + prod[2 * shots :]
-        prod = prod + jnp.dot(xr[: 2 * shots, :], wr[j, :, 2 * LB :], preferred_element_type=F32)
-        re = prod[:shots, :LB] - prod[shots:, LB:]
-        im = prod[:shots, LB:] + prod[shots:, :LB]
-        row = jnp.sum(ff[0, :, cols] * re + ff[1, :, cols] * im, axis=0, keepdims=True)
-        gbuf[pl.ds(j, 1), :] = row * (shots ** (-0.5))
-        return carry
+            xr[h, part_no * half : (part_no + 1) * half, first_col : first_col + width] = high
+            xr[h, (2 + part_no) * half : (3 + part_no) * half, first_col : first_col + width] = low
 
     neb = gbuf.shape[0]
-    lax.fori_loop(0, neb, recover, 0)
-
-    grads = gbuf[...]
+
+    def recover(h):
+        rows = pl.ds(half * h, half)
+        place(h, ubuf[core, :, rows, :], LB)
+        place(h, lext[:, rows, :], 0)
+        place(h, rext[:, rows, :], LB + trace)
+
+        def block(j, carry):
+            cols = pl.ds(pl.multiple_of(j * LB, LB), LB)
+            prod = jnp.dot(xr[h], wr[j, :, : 2 * LB], preferred_element_type=F32)
+            prod = prod[: 2 * half] + prod[2 * half :]
+            prod = prod + jnp.dot(xr[h, : 2 * half, :], wr[j, :, 2 * LB :], preferred_element_type=F32)
+            re = prod[:half, :LB] - prod[half:, LB:]
+            im = prod[:half, LB:] + prod[half:, :LB]
+            row = jnp.sum(ff[0, rows, cols] * re + ff[1, rows, cols] * im, axis=0, keepdims=True)
+            if h == 0:
+                gbuf[pl.ds(j, 1), :] = row
+            else:
+                gbuf[pl.ds(j, 1), :] = gbuf[pl.ds(j, 1), :] + row
+            return carry
+
+        lax.fori_loop(0, neb, block, 0)
+
+    arrive(0)
+    recover(0)
+    arrive(1)
+    leave = pltpu.make_async_copy(ubuf.at[core], u_hbm, load_sem.at[6])
+    leave.start()
+    recover(1)
+
+    grads = gbuf[...] * (shots ** (-0.5))
     lanes = lax.broadcasted_iota(jnp.int32, gsend.shape[1:], 0)
     placed = []
     for b in range(neb):
@@ -534,7 +564,7 @@
         gsend[s] = total
 
     def grad_copy(to, sender):
-        return remote(gsend.at[to], grecv.at[sender], gs_.at[to], gr_.at[sender], "slab", to)
+        return remote(gsend.at[to], grecv.at[sender], gs_, gr_, "slab", to)
 
     def grad_send(k, carry):
         grad_copy(lax.rem(me + k, slabs), me).start()
@@ -543,47 +573,41 @@
     lax.fori_loop(1, slabs, grad_send, 0)
     grecv[me] = gsend[me]
 
-    def drain1(i, carry):
-        for col in (0, 1):
-            s = slab_at(col, lax.rem(ring(col) + 2, RY), i)
-            for way in (0, 1):
-                half_copy(1, col, i, way, s).wait_send()
-                full_copy(1, col, i, way, s).wait_send()
-        return carry
-
-    lax.fori_loop(0, RY, drain1, 0)
-    for col in (0, 1):
-        for way in (0, 1):
-            half_copy(2, col, 0, way, me).wait_send()
-            full_copy(2, col, 0, way, me).wait_send()
-
-    def drain2(c, carry):
-        for w in (0, 1):
-
-            @pl.when(me < slabs - 1)
-            def _():
-                down_copy(c, w).wait_send()
-
-            @pl.when(me > 0)
-            def _():
-                up_copy(c, w).wait_send()
-
-        back_copy(c).wait_send()
-        first_cells(c, 1, mate).wait_send()
+    def sent(ref, sem, axis="slab", where=me):
+        remote(ref, ref, sem, sem, axis, where).wait_send()
+
+    sent(h1, h1s)
+    sent(f1, f1s)
+    sent(h2, h2s)
+    sent(f2, f2s)
+
+    @pl.when(core == 1)
+    def _():
+        sent(dbuf, ds_)
+        sent(ubuf, us_)
+
+        @pl.when(me == 0)
+        def _():
+            for w in (0, 1):
+                for c in range(nch):
+                    down_copy(c, w).wait_recv()
+
+        @pl.when(me == slabs - 1)
+        def _():
+            for w in (0, 1):
+                for c in range(nch):
+                    up_copy(c, w).wait_recv()
+
+        sent(ubuf.at[0], as_)
+        sent(rext, rs_)
 
         @pl.when(lat > 1)
         def _():
-            first_cells(c, 0, before2).wait_send()
+            sent(rext, r2s_)
 
         @pl.when(lat < lats - 1)
         def _():
-            last_cells(c, 1, after).wait_send()
-
-        return carry
-
-    @pl.when(core == 1)
-    def _():
-        lax.fori_loop(0, nch, drain2, 0)
+            sent(lext, ls_)
 
     @pl.when(core == 0)
     def _():
@@ -591,18 +615,14 @@
             panel_copy(k).wait_send()
             source_copy(k).wait_send()
 
-    def grad_wait(k, total):
-        other = lax.rem(me + k, slabs)
-        grad_copy(other, other).wait_recv()
-        return total + grecv[other]
-
-    model_out[...] = lax.fori_loop(1, slabs, grad_wait, grecv[me])
-
-    def grad_drain(k, carry):
-        grad_copy(lax.rem(me + k, slabs), me).wait_send()
-        return carry
-
-    lax.fori_loop(1, slabs, grad_drain, 0)
+    leave.wait()
+    all_others = pl.ds(0, slabs - 1)
+    remote(gsend.at[all_others], grecv.at[all_others], gs_, gr_, "slab", me).wait_recv()
+    total = grecv[0]
+    for k in range(1, slabs):
+        total = total + grecv[k]
+    model_out[...] = total
+    sent(gsend.at[all_others], gs_)
 
 
 def body(
@@ -635,8 +655,8 @@
             jax.ShapeDtypeStruct((2, shots, trace), F32),
             jax.ShapeDtypeStruct((neb, width), F32),
         ),
-        in_specs=[smem] * 4 + [vmem] * 2 + [hbm] * 5,
-        out_specs=(vmem, vmem),
+        in_specs=[vmem] * 2 + [smem] * 4 + [hbm] * 5,
+        out_specs=(hbm, vmem),
         scratch_shapes=[
             pltpu.VMEM((nres, 2, shots, width), F32),
             pltpu.VMEM((4, 2, trace, trace), F32),
@@ -657,32 +677,35 @@
             pltpu.VMEM((2, 2, shots, trace), F32),
             pltpu.VMEM((2, shots, width), F32),
             pltpu.VMEM((2, shots, width), F32),
-            pltpu.VMEM((4 * shots, depth), BF16),
+            pltpu.VMEM((2, 2 * shots, depth), BF16),
             pltpu.VMEM((neb, width), F32),
             pltpu.VMEM((slabs, neb, width), F32),
             pltpu.VMEM((slabs, neb, width), F32),
-            dma((5,)),
+            pltpu.VMEM((slabs, width), jnp.int32),
+            pltpu.SMEM((slabs, width), jnp.int32),
+            pltpu.VMEM((2, shots, width), F32),
+            dma((7,)),
+            dma,
             dma((2, RY, 2)),
+            dma,
             dma((2, RY, 2)),
-            dma((2, RY, 2)),
-            dma((2, RY, 2)),
+            dma,
             dma((2, 2)),
+            dma,
             dma((2, 2)),
-            dma((2, 2)),
-            dma((2, 2)),
+            dma,
             dma((2, nch)),
+            dma,
             dma((2, nch)),
-            dma((2, nch)),
-            dma((2, nch)),
-            dma((nch,)),
-            dma((nch,)),
-            dma((nch,)),
-            dma((nch,)),
-            dma((nch,)),
-            dma((nch,)),
-            dma((nch,)),
-            dma((slabs,)),
-            dma((slabs,)),
+            dma,
+            dma((2,)),
+            dma,
+            dma,
+            dma((2,)),
+            dma,
+            dma((2,)),
+            dma,
+            dma,
             dma((2,)),
             dma((2,)),
             dma((2,)),
@@ -692,12 +715,12 @@
             collective_id=0, has_side_effects=True, vmem_limit_bytes=60 * 1024 * 1024
         ),
     )(
-        residual_slab.reshape(-1),
-        residual_pos,
+        residual_slab.reshape(1, -1),
+        residual_pos.reshape(1, -1),
         element_owner.reshape(-1),
         element_slot,
-        shot_ids.reshape(-1, 1),
-        wavelet,
+        shot_ids,
+        wavelet.T,
         residual_blocks,
         down_panel[0, 0],
         up_panel[0, 0],

time: 145 us -> 138 us (0.952)
  Pallas kernels: 139 us -> 135 us
  local copies, waits for them, and re-layouts: 5.67 us -> 2.95 us
    pallas_call x1, Pallas kernels: 139 us -> 135 us  [body(): pl.pallas_call(kernel, out_shape=(jax.ShapeDtypeStruct((2, shots, trace),...]
    unnamed x3 -> x2, local copies, waits for them, and re-layouts: 4.31 us -> 2.95 us
where the time goes in v3:
time: 138 us
  Pallas kernels  135 us (98%)
  local copies, waits for them, and re-layouts  2.95 us (2%)
    pallas_call x1, Pallas kernels, body(): pl.pallas_call(kernel, out_shape=(jax.ShapeDtypeStruct((2, shots, trace),...  135 us
    unnamed x2, local copies, waits for them, and re-layouts  2.95 us

profile of v3, /device:TPU:1, one launch (start us, length us, event | category | flops | bytes accessed | tf_op | source)
XLA Modules:
  0.0 138.2 jit_solution(12617816702613386139)
XLA Ops:
  0.6 134.6 %shard_map.122 = (f32[2,64,512]{2,1,0:T(8,128)}, f32[8,128]{1,0:T(8,128)}) custom-call(s32[1,32]{1,0:T(1,128)} %bitcast.17, s32[1,32]{1,0:T(1,128)} %bitcast.18, s32[8]{0:T(128)} %bitcast.19, s32[8]{0:T(128)} %slot_sm.1, s32[64]{0:T(128)} %shot_sm.1, f32[2,64]{1,0:T(2,128)} %bitcast.16, f32[32,2,64,128]{3,2,1,0:T(8,128)} %res_hbm.1, ...), custom_call_target="tpu_custom_call" | custom-call | tf_op jit(solution)/shard_map/pallas_call | solution.py:652
  135.3 1.7 %copy.15 = f32[1,1,2,64,512]{4,3,2,1,0:T(8,128)} copy(f32[1,1,2,64,512]{4,3,2,1,0:T(8,128)} %bitcast.14) | data formatting | bytes 524288
  136.9 1.3 copy.16

commit v4 on v3

--- a/solution.py
+++ b/solution.py
@@ -14,7 +14,8 @@
 RY = 4
 CAP = 4
 CH = 8
-NS = 1
+VR = 32
+VP = 64
 
 
 def split(value):
@@ -53,7 +54,7 @@
     rec,
     ff,
     wd,
-    wu,
+    wz,
     wr,
     part,
     h1,
@@ -61,7 +62,7 @@
     h2,
     f2,
     src,
-    dbuf,
+    de,
     ubuf,
     drecv,
     urecv,
@@ -74,6 +75,9 @@
     tab_v,
     tab_sm,
     wbuf,
+    upan,
+    vland,
+    erecv,
     load_sem,
     h1s,
     h1r,
@@ -100,6 +104,13 @@
     pr_,
     ss_,
     sr_,
+    ul_,
+    vs_,
+    vr_,
+    xs_,
+    xr_,
+    es_,
+    er_,
 ):
     slabs = 16
     lats = 8
@@ -115,6 +126,12 @@
 
     core = lax.rem(lat, 2)
     mate = lat + 1 - 2 * core
+    top = slabs - RY
+    even = lax.rem(me, 2) == 0
+    pair = jnp.logical_and(even, me < top)
+    leaf = jnp.logical_and(lax.rem(me, 2) == 1, me < top)
+    which = jnp.where(pair, 1, 0)
+    below = lax.rem(me + slabs - 1, slabs)
     load_res = pltpu.make_async_copy(res_hbm, res, load_sem.at[0])
     load_down = pltpu.make_async_copy(down_hbm, pan.at[0], load_sem.at[1])
     load_up = pltpu.make_async_copy(up_hbm, pan.at[1], load_sem.at[2])
@@ -125,6 +142,9 @@
     @pl.when(core == 1)
     def _():
         load_down.start()
+
+    @pl.when(jnp.logical_or(core == 1, pair))
+    def _():
         load_up.start()
 
     load_rec.start()
@@ -323,17 +343,31 @@
             part[s, way, rows, :] = part[s, way, rows, :] + h2[col, way]
             full_copy(2, col, i, way, s).start()
 
+    def piece_copy(b):
+        rows = pl.ds(pl.multiple_of(b * VP, VP), VP)
+        return remote(up_hbm.at[:, rows, :], upan.at[:, rows, :], vs_, vr_.at[b], "slab", below)
+
+    @pl.when(leaf)
+    def _():
+        for b in range(trace // VP):
+            piece_copy(b).start()
+
     @pl.when(core == 1)
     def _():
         panel_copy(0).wait_recv()
         pack(pan, 2, wd.at[0], trace // LB)
         load_up.wait()
-        pack(pan, 1, wu.at[1], trace // LB)
+        pack(pan, 1, wz.at[0, 1], trace // LB)
 
     @pl.when(core == 0)
     def _():
         load_rec.wait()
         pack(rec, None, wr, rec.shape[2] // LB)
+
+        @pl.when(pair)
+        def _():
+            load_up.wait()
+            pack(pan, 1, wz.at[0, 0], trace // LB)
 
     @pl.when(lat == 0)
     def _():
@@ -361,51 +395,41 @@
         def _():
             source_copy(col).start()
 
-    def turn(arrived, target, rows, weight, extra, piece):
-        x = jnp.concatenate([arrived[0, rows, :], arrived[1, rows, :]], axis=0)
-        high, low = split(x)
+    def product(first, second, weight, j):
+        count = first.shape[0]
+        high, low = split(jnp.concatenate([first, second], axis=0))
         x = jnp.concatenate([high, low], axis=0)
-        count = trace // LB
-        group = count // NS
-        prods = [jnp.dot(x, weight[j], preferred_element_type=F32) for j in range(min(group + 1, count))]
-        for k in range(NS):
-            for j in range(k * group, (k + 1) * group):
-                cols = slice(j * LB, (j + 1) * LB)
-                prod = prods[j][: 2 * CH] + prods[j][2 * CH :]
-                prod = prod[:, : 2 * LB] + prod[:, 2 * LB :]
-                target[0, rows, cols] = prod[:CH, :LB] - prod[CH:, LB:] + extra[0, rows, cols]
-                target[1, rows, cols] = prod[:CH, LB:] + prod[CH:, :LB] + extra[1, rows, cols]
-            piece(k).start()
-            for j in range(len(prods), min(len(prods) + group, count)):
-                prods.append(jnp.dot(x, weight[j], preferred_element_type=F32))
+        prod = jnp.dot(x, weight[j], preferred_element_type=F32)
+        prod = prod[: 2 * count] + prod[2 * count :]
+        prod = prod[:, : 2 * LB] + prod[:, 2 * LB :]
+        return prod[:count, :LB] - prod[count:, LB:], prod[:count, LB:] + prod[count:, :LB]
+
+    def turn(arrived, target, rows, weight, extra):
+        first, second = arrived[0, rows, :], arrived[1, rows, :]
+        for j in range(trace // LB):
+            cols = slice(j * LB, (j + 1) * LB)
+            re, im = product(first, second, weight, j)
+            target[0, rows, cols] = re + extra[0, rows, cols]
+            target[1, rows, cols] = im + extra[1, rows, cols]
 
     def rows_of(c):
         return pl.ds(pl.multiple_of(c * CH, CH), CH)
 
-    def cols_of(k):
-        return pl.ds(0, trace) if k is None else pl.ds(k * (trace // NS), trace // NS)
-
-    def down_copy(c, w, k=None):
-        rows, cols = rows_of(c), cols_of(k)
+    def down_copy(c, w):
+        rows = rows_of(c)
         return remote(
-            dbuf.at[w, :, rows, cols],
-            drecv.at[w, :, rows, cols],
-            ds_,
-            dr_.at[w, c],
-            "slab",
-            lax.rem(me + 1, slabs),
+            de.at[0, w, :, rows, :], drecv.at[w, :, rows, :], ds_, dr_.at[w, c], "slab", lax.rem(me + 1, slabs)
         )
 
-    def up_copy(c, w, k=None):
-        rows, cols = rows_of(c), cols_of(k)
-        return remote(
-            ubuf.at[w, :, rows, cols],
-            urecv.at[w, :, rows, cols],
-            us_,
-            ur_.at[w, c],
-            "slab",
-            lax.rem(me + slabs - 1, slabs),
-        )
+    has_chain = jnp.logical_or(me > top, jnp.logical_and(even, me > 0))
+    has_leaf = jnp.logical_and(even, jnp.logical_and(me > 0, me <= top))
+
+    def up_copy(c, w, to_leaf=False):
+        rows = rows_of(c)
+        step = jnp.where(me > top, 1, 2)
+        to = below if to_leaf else lax.rem(me + slabs - step, slabs)
+        send = ul_ if to_leaf else us_
+        return remote(ubuf.at[w, :, rows, :], urecv.at[w, :, rows, :], send, ur_.at[w, c], "slab", to)
 
     def last_cells(rows, w, h, to):
         return remote(
@@ -426,6 +450,14 @@
         rows = rows_of(c)
         h = lax.div(c, nch // 2)
 
+        @pl.when(has_chain)
+        def _():
+            up_copy(c, w).start()
+
+        @pl.when(has_leaf)
+        def _():
+            up_copy(c, w, True).start()
+
         if w == 0:
             back_copy(rows, h).start()
 
@@ -447,18 +479,20 @@
 
             @pl.when(me == 0)
             def _():
-                dbuf[w, :, rows, :] = src[w, :, rows, :]
-                down_copy(c, w).start()
+                de[0, w, :, rows, :] = src[w, :, rows, :]
 
             @pl.when(me > 0)
             def _():
                 down_copy(c, w).wait_recv()
-                turn(drecv.at[w], dbuf.at[w], rows, wd.at[w], src.at[w], lambda k: down_copy(c, w, k))
+                turn(drecv.at[w], de.at[0, w], rows, wd.at[w], src.at[w])
+
+            @pl.when(me < slabs - 1)
+            def _():
+                down_copy(c, w).start()
 
             @pl.when(me == slabs - 1)
             def _():
-                ubuf[w, :, rows, :] = dbuf[w, :, rows, :]
-                up_copy(c, w).start()
+                ubuf[w, :, rows, :] = de[0, w, :, rows, :]
                 finish(c, w)
 
         return carry
@@ -467,13 +501,52 @@
         rows = rows_of(c)
         for w in (1, 0):
             up_copy(c, w).wait_recv()
-            turn(urecv.at[w], ubuf.at[w], rows, wu.at[w], dbuf.at[w], lambda k: up_copy(c, w, k))
+            turn(urecv.at[w], ubuf.at[w], rows, wz.at[which, w], de.at[which, w])
             finish(c, w)
         return carry
 
+    def give_copy(b):
+        rows = pl.ds(pl.multiple_of(b * VP, VP), VP)
+        return remote(vland.at[:, rows, :], vland.at[:, rows, :], xs_, xr_, "lat", mate)
+
+    def form(store, done):
+        def piece(b, carry):
+            piece_copy(b).wait_recv()
+
+            def block(k, carry):
+                rows = pl.ds(pl.multiple_of(b * VP + k * VR, VR), VR)
+                first, second = upan[0, rows, :], upan[1, rows, :]
+                for j in range(trace // LB):
+                    re, im = product(first, second, wz.at[0, core], j)
+                    store(j, rows, re, im)
+                return carry
+
+            lax.fori_loop(0, VP // VR, block, 0)
+            done(b)
+            return carry
+
+        lax.fori_loop(0, trace // VP, piece, 0)
+
+    def store_packed(j, rows, re, im):
+        for part_no, value in enumerate((re, im)):
+            high, low = split(value)
+            wz[1, 1, j, rows, part_no * LB : (part_no + 1) * LB] = high
+            wz[1, 1, j, rows, (2 + part_no) * LB : (3 + part_no) * LB] = low
+
+    def store_plain(j, rows, re, im):
+        vland[0, rows, j * LB : (j + 1) * LB] = re
+        vland[1, rows, j * LB : (j + 1) * LB] = im
+
+    def odd_copy(w):
+        return remote(de.at[0, w], erecv.at[w], es_, er_.at[w], "slab", below)
+
+    @pl.when(jnp.logical_and(core == 0, pair))
+    def _():
+        form(store_plain, lambda b: give_copy(b).start())
+
     def late_packs():
         panel_copy(1).wait_recv()
-        pack(pan, 3, wu.at[0], trace // LB)
+        pack(pan, 3, wz.at[0, 0], trace // LB)
         load_rec.wait()
         pack(rec, None, wr, rec.shape[2] // LB)
 
@@ -487,9 +560,29 @@
             source_copy(col).wait_recv()
         lax.fori_loop(0, nch, down, 0)
 
+        @pl.when(leaf)
+        def _():
+            for w in (1, 0):
+                odd_copy(w).start()
+
         @pl.when(me < slabs // 2)
         def _():
             late_packs()
+
+        @pl.when(pair)
+        def _():
+            form(store_packed, lambda b: None)
+            remote(vland, vland, xs_, xr_, "lat", mate).wait_recv()
+            pack(vland, None, wz.at[1, 0], trace // LB)
+            for w in (1, 0):
+                odd_copy(w).wait_recv()
+
+                def two(k, carry):
+                    rows = pl.ds(pl.multiple_of(k * VR, VR), VR)
+                    turn(erecv.at[w], de.at[1, w], rows, wz.at[0, w], de.at[0, w])
+                    return carry
+
+                lax.fori_loop(0, shots // VR, two, 0)
 
         @pl.when(me < slabs - 1)
         def _():
@@ -576,6 +669,14 @@
     def sent(ref, sem, axis="slab", where=me):
         remote(ref, ref, sem, sem, axis, where).wait_send()
 
+    @pl.when(leaf)
+    def _():
+        sent(upan, vs_)
+
+    @pl.when(jnp.logical_and(core == 0, pair))
+    def _():
+        sent(vland, xs_)
+
     sent(h1, h1s)
     sent(f1, f1s)
     sent(h2, h2s)
@@ -583,20 +684,21 @@
 
     @pl.when(core == 1)
     def _():
-        sent(dbuf, ds_)
-        sent(ubuf, us_)
-
-        @pl.when(me == 0)
-        def _():
-            for w in (0, 1):
-                for c in range(nch):
-                    down_copy(c, w).wait_recv()
-
-        @pl.when(me == slabs - 1)
-        def _():
-            for w in (0, 1):
-                for c in range(nch):
-                    up_copy(c, w).wait_recv()
+        @pl.when(me < slabs - 1)
+        def _():
+            sent(de.at[0], ds_)
+
+        @pl.when(has_chain)
+        def _():
+            sent(ubuf, us_)
+
+        @pl.when(has_leaf)
+        def _():
+            sent(ubuf, ul_)
+
+        @pl.when(leaf)
+        def _():
+            sent(de.at[0], es_)
 
         sent(ubuf.at[0], as_)
         sent(rext, rs_)
@@ -663,7 +765,7 @@
             pltpu.VMEM((2, depth, nel), F32),
             pltpu.VMEM((2, shots, nel), F32),
             pltpu.VMEM((2, trace // width, trace, 4 * width), BF16),
-            pltpu.VMEM((2, trace // width, trace, 4 * width), BF16),
+            pltpu.VMEM((2, 2, trace // width, trace, 4 * width), BF16),
             pltpu.VMEM((nel // width, depth, 4 * width), BF16),
             pltpu.VMEM((slabs, 2, shots, trace), F32),
             pltpu.VMEM((2, RY, 2, half, trace), F32),
@@ -671,7 +773,7 @@
             pltpu.VMEM((2, 2, half, trace), F32),
             pltpu.VMEM((2, 2, 2, half, trace), F32),
             pltpu.VMEM((2, 2, shots, trace), F32),
-            pltpu.VMEM((2, 2, shots, trace), F32),
+            pltpu.VMEM((2, 2, 2, shots, trace), F32),
             pltpu.VMEM((2, 2, shots, trace), F32),
             pltpu.VMEM((2, 2, shots, trace), F32),
             pltpu.VMEM((2, 2, shots, trace), F32),
@@ -684,6 +786,9 @@
             pltpu.VMEM((slabs, width), jnp.int32),
             pltpu.SMEM((slabs, width), jnp.int32),
             pltpu.VMEM((2, shots, width), F32),
+            pltpu.VMEM((2, trace, trace), F32),
+            pltpu.VMEM((2, trace, trace), F32),
+            pltpu.VMEM((2, 2, shots, trace), F32),
             dma((7,)),
             dma,
             dma((2, RY, 2)),
@@ -709,6 +814,13 @@
             dma((2,)),
             dma((2,)),
             dma((2,)),
+            dma((2,)),
+            dma,
+            dma,
+            dma((trace // VP,)),
+            dma,
+            dma,
+            dma,
             dma((2,)),
         ],
         compiler_params=pltpu.CompilerParams(

time: 138 us -> 127 us (0.920)
  Pallas kernels: 135 us -> 123 us
    pallas_call x1, Pallas kernels: 135 us -> 123 us  [body(): pl.pallas_call(kernel, out_shape=(jax.ShapeDtypeStruct((2, shots, trace),...]
where the time goes in v4:
time: 127 us
  Pallas kernels  123 us (97%)
  local copies, waits for them, and re-layouts  2.95 us (2%)
    pallas_call x1, Pallas kernels, body(): pl.pallas_call(kernel, out_shape=(jax.ShapeDtypeStruct((2, shots, trace),...  123 us
    unnamed x2, local copies, waits for them, and re-layouts  2.95 us

profile of v4, /device:TPU:1, one launch (start us, length us, event | category | flops | bytes accessed | tf_op | source)
XLA Modules:
  0.0 127.0 jit_solution(3345410370055041930)
XLA Ops:
  0.6 123.4 %shard_map.122 = (f32[2,64,512]{2,1,0:T(8,128)}, f32[8,128]{1,0:T(8,128)}) custom-call(s32[1,32]{1,0:T(1,128)} %bitcast.17, s32[1,32]{1,0:T(1,128)} %bitcast.18, s32[8]{0:T(128)} %bitcast.19, s32[8]{0:T(128)} %slot_sm.1, s32[64]{0:T(128)} %shot_sm.1, f32[2,64]{1,0:T(2,128)} %bitcast.16, f32[32,2,64,128]{3,2,1,0:T(8,128)} %res_hbm.1, ...), custom_call_target="tpu_custom_call" | custom-call | tf_op jit(solution)/shard_map/pallas_call | solution.py:754
  124.1 1.7 %copy.15 = f32[1,1,2,64,512]{4,3,2,1,0:T(8,128)} copy(f32[1,1,2,64,512]{4,3,2,1,0:T(8,128)} %bitcast.14) | data formatting | bytes 524288
  125.7 1.3 %copy.16 = f32[1,1,8,128]{3,2,1,0:T(8,128)} copy(f32[1,1,8,128]{3,2,1,0:T(8,128)} %bitcast.15) | data formatting | bytes 8192

commit v5 on v4

--- a/solution.py
+++ b/solution.py
@@ -250,7 +250,7 @@
             build(col, s)
         return carry
 
-    lax.fori_loop(0, RY, first, 0)
+    first(0, 0)
     peers = 4 + (lat > 0).astype(jnp.int32) + (lat < lats - 1).astype(jnp.int32)
     peers = peers + core * ((lat > 1).astype(jnp.int32) + (lat < lats - 1).astype(jnp.int32))
     pl.semaphore_wait(barrier, peers)
@@ -271,7 +271,22 @@
                 half_copy(1, col, i, way, s).start()
         return carry
 
-    lax.fori_loop(0, RY, first_send, 0)
+    first_send(0, 0)
+
+    def first_rest(k, carry):
+        first(k, carry)
+        return first_send(k, carry)
+
+    lax.fori_loop(1, RY, first_rest, 0)
+
+    def middle(k, carry):
+        for col in (0, 1):
+            i = order(col, k)
+            for step in (RY - 1, 1, 0):
+                build(col, slab_at(col, lax.rem(ring(col) + step, RY), i))
+        return carry
+
+    lax.fori_loop(0, RY, middle, 0)
 
     def second(k, carry):
         for col in (0, 1):
@@ -280,20 +295,29 @@
                 t = lax.rem(ring(col) + (RY - 1 if way == 0 else 1), RY)
                 s = slab_at(col, t, i)
                 rows = pl.ds(half * col, half)
-                build(col, s)
                 half_copy(1, col, i, way, s).wait_recv()
                 part[s, way, rows, :] = part[s, way, rows, :] + h1[col, i, way]
                 full_copy(1, col, i, way, s).start()
         return carry
 
-    lax.fori_loop(0, RY, second, 0)
-
-    def own(i, carry):
+    def gather(k, carry):
         for col in (0, 1):
-            build(col, slab_at(col, ring(col), i))
+            i = order(col, k)
+            s = slab_at(col, ring(col), i)
+            rows = pl.ds(half * col, half)
+            for way in (0, 1):
+                full_copy(1, col, i, way, s).wait_recv()
+            part[s, :, rows, :] = part[s, :, rows, :] + (f1[col, i, 0] + f1[col, i, 1])
         return carry
 
-    lax.fori_loop(0, RY, own, 0)
+    lax.fori_loop(0, 2, second, 0)
+    gather(0, 0)
+    for col in (0, 1):
+        i = lax.rem(cross(col) + 2, RY)
+        s = slab_at(col, ring(col), i)
+        for way in (0, 1):
+            half_copy(2, col, i, way, s).start()
+    lax.fori_loop(2, RY, second, 0)
 
     def pack(source, which, target, count):
         def col_block(j, carry):
@@ -317,23 +341,7 @@
         panel_copy(1).start()
 
 
-    def gather(k, carry):
-        for col in (0, 1):
-            i = order(col, k)
-            s = slab_at(col, ring(col), i)
-            rows = pl.ds(half * col, half)
-            for way in (0, 1):
-                full_copy(1, col, i, way, s).wait_recv()
-            part[s, :, rows, :] = part[s, :, rows, :] + (f1[col, i, 0] + f1[col, i, 1])
-        return carry
-
-    lax.fori_loop(0, 1, gather, 0)
-    for col in (0, 1):
-        i = lax.rem(cross(col) + 2, RY)
-        s = slab_at(col, ring(col), i)
-        for way in (0, 1):
-            half_copy(2, col, i, way, s).start()
-    lax.fori_loop(1, RY, gather, 0)
+    lax.fori_loop(1, RY - 1, gather, 0)
     for col in (0, 1):
         rows = pl.ds(half * col, half)
         for way in (0, 1):
@@ -342,6 +350,7 @@
             half_copy(2, col, i, way, s).wait_recv()
             part[s, way, rows, :] = part[s, way, rows, :] + h2[col, way]
             full_copy(2, col, i, way, s).start()
+    gather(RY - 1, 0)
 
     def piece_copy(b):
         rows = pl.ds(pl.multiple_of(b * VP, VP), VP)
@@ -615,11 +624,20 @@
 
     neb = gbuf.shape[0]
 
+    depth = xr.shape[-1]
+
+    def put_all(h, rim):
+        rows = pl.ds(half * h, half)
+        if rim:
+            place(h, rext[:, rows, :], LB + trace)
+        else:
+            place(h, ubuf[core, :, rows, :], LB)
+            place(h, lext[:, rows, :], 0)
+
     def recover(h):
+        put_all(h, False)
+        put_all(h, True)
         rows = pl.ds(half * h, half)
-        place(h, ubuf[core, :, rows, :], LB)
-        place(h, lext[:, rows, :], 0)
-        place(h, rext[:, rows, :], LB + trace)
 
         def block(j, carry):
             cols = pl.ds(pl.multiple_of(j * LB, LB), LB)
@@ -637,12 +655,40 @@
 
         lax.fori_loop(0, neb, block, 0)
 
-    arrive(0)
-    recover(0)
-    arrive(1)
     leave = pltpu.make_async_copy(ubuf.at[core], u_hbm, load_sem.at[6])
-    leave.start()
-    recover(1)
+
+    @pl.when(core == 0)
+    def _():
+        arrive(0)
+        recover(0)
+        arrive(1)
+        leave.start()
+        recover(1)
+
+    @pl.when(core == 1)
+    def _():
+        leave.start()
+        for h in (0, 1):
+            put_all(h, False)
+        for h in (0, 1):
+            arrive(h)
+            put_all(h, True)
+
+        def block(j, carry):
+            cols = pl.ds(pl.multiple_of(j * LB, LB), LB)
+            prod = jnp.dot(xr[...].reshape(4 * shots, depth), wr[j], preferred_element_type=F32)
+            prod = prod[:, : 2 * LB] + prod[:, 2 * LB :]
+            row = jnp.zeros((1, LB), F32)
+            for h in (0, 1):
+                rows = pl.ds(half * h, half)
+                part_sum = prod[2 * shots * h : 2 * shots * h + shots] + prod[2 * shots * h + shots : 2 * shots * (h + 1)]
+                re = part_sum[:half, :LB] - part_sum[half:, LB:]
+                im = part_sum[:half, LB:] + part_sum[half:, :LB]
+                row = row + jnp.sum(ff[0, rows, cols] * re + ff[1, rows, cols] * im, axis=0, keepdims=True)
+            gbuf[pl.ds(j, 1), :] = row
+            return carry
+
+        lax.fori_loop(0, neb, block, 0)
 
     grads = gbuf[...] * (shots ** (-0.5))
     lanes = lax.broadcasted_iota(jnp.int32, gsend.shape[1:], 0)
@@ -725,6 +771,11 @@
         total = total + grecv[k]
     model_out[...] = total
     sent(gsend.at[all_others], gs_)
+
+
+def deliver(u_ref, model_ref, u_out, model_out):
+    u_out[...] = u_ref[...]
+    model_out[...] = model_ref[...]
 
 
 def body(
@@ -839,6 +890,15 @@
         recovery[0, 0],
         forward_field[0, 0],
     )
+    ups, model = pl.pallas_call(
+        deliver,
+        out_shape=(
+            jax.ShapeDtypeStruct((2, shots, trace), F32),
+            jax.ShapeDtypeStruct((neb, width), F32),
+        ),
+        in_specs=[vmem, vmem],
+        out_specs=(vmem, vmem),
+    )(ups, model)
     return (ups[None, None], model[None, None])
 
 

time: 127 us -> 125 us (0.984)
  local copies, waits for them, and re-layouts: 2.95 us -> 0 us
    unnamed x2 -> x0, local copies, waits for them, and re-layouts: 2.95 us -> none
    pallas_call x0 -> x1, Pallas kernels: none -> 1.68 us  [body(): pl.pallas_call(deliver, out_shape=(jax.ShapeDtypeStruct((2, shots, trace)...]
where the time goes in v5:
time: 125 us
  Pallas kernels  124 us (99%)
    pallas_call x1, Pallas kernels, body(): pl.pallas_call(kernel, out_shape=(jax.ShapeDtypeStruct((2, shots, trace),...  123 us

profile of v5, /device:TPU:1, one launch (start us, length us, event | category | flops | bytes accessed | tf_op | source)
XLA Modules:
  0.0 125.0 jit_solution(7689908672654933565)
XLA Ops:
  0.6 122.6 %shard_map.122 = (f32[2,64,512]{2,1,0:T(8,128)}, f32[8,128]{1,0:T(8,128)}) custom-call(s32[1,32]{1,0:T(1,128)} %bitcast.15, s32[1,32]{1,0:T(1,128)} %bitcast.16, s32[8]{0:T(128)} %bitcast.17, s32[8]{0:T(128)} %slot_sm.1, s32[64]{0:T(128)} %shot_sm.1, f32[2,64]{1,0:T(2,128)} %bitcast.14, f32[32,2,64,128]{3,2,1,0:T(8,128)} %res_hbm.1, ...), custom_call_target="tpu_custom_call" | custom-call | tf_op jit(solution)/shard_map/pallas_call | solution.py:805
  123.3 1.7 %shard_map.123 = (f32[2,64,512]{2,1,0:T(8,128)}, f32[8,128]{1,0:T(8,128)}) custom-call(f32[2,64,512]{2,1,0:T(8,128)} %get-tuple-element.6.u_ref, f32[8,128]{1,0:T(8,128)} %get-tuple-element.7.model_ref), custom_call_target="tpu_custom_call" | custom-call | tf_op jit(solution)/shard_map/pallas_call | solution.py:893

commit v6 on v5

--- a/solution.py
+++ b/solution.py
@@ -484,7 +484,7 @@
 
     def down(c, carry):
         rows = rows_of(c)
-        for w in (1, 0):
+        for w in (0, 1):
 
             @pl.when(me == 0)
             def _():
@@ -508,7 +508,7 @@
 
     def up(c, carry):
         rows = rows_of(c)
-        for w in (1, 0):
+        for w in (0, 1):
             up_copy(c, w).wait_recv()
             turn(urecv.at[w], ubuf.at[w], rows, wz.at[which, w], de.at[which, w])
             finish(c, w)
@@ -518,7 +518,7 @@
         rows = pl.ds(pl.multiple_of(b * VP, VP), VP)
         return remote(vland.at[:, rows, :], vland.at[:, rows, :], xs_, xr_, "lat", mate)
 
-    def form(store, done):
+    def form(store, done, start, stop):
         def piece(b, carry):
             piece_copy(b).wait_recv()
 
@@ -534,7 +534,7 @@
             done(b)
             return carry
 
-        lax.fori_loop(0, trace // VP, piece, 0)
+        lax.fori_loop(start, stop, piece, 0)
 
     def store_packed(j, rows, re, im):
         for part_no, value in enumerate((re, im)):
@@ -551,7 +551,7 @@
 
     @pl.when(jnp.logical_and(core == 0, pair))
     def _():
-        form(store_plain, lambda b: give_copy(b).start())
+        form(store_plain, lambda b: give_copy(b).start(), 0, trace // VP)
 
     def late_packs():
         panel_copy(1).wait_recv()
@@ -567,6 +567,12 @@
 
         for col in (0, 1):
             source_copy(col).wait_recv()
+        early = jnp.where(jnp.logical_and(pair, me >= slabs // 2), trace // VP // 2, 0)
+
+        @pl.when(pair)
+        def _():
+            form(store_packed, lambda b: None, 0, early)
+
         lax.fori_loop(0, nch, down, 0)
 
         @pl.when(leaf)
@@ -580,7 +586,7 @@
 
         @pl.when(pair)
         def _():
-            form(store_packed, lambda b: None)
+            form(store_packed, lambda b: None, early, trace // VP)
             remote(vland, vland, xs_, xr_, "lat", mate).wait_recv()
             pack(vland, None, wz.at[1, 0], trace // LB)
             for w in (1, 0):

time: 125 us -> 123 us (0.984)
  Pallas kernels: 124 us -> 122 us
    pallas_call x1, Pallas kernels: 123 us -> 121 us  [body(): pl.pallas_call(kernel, out_shape=(jax.ShapeDtypeStruct((2, shots, trace),...]
where the time goes in v6:
time: 123 us
  Pallas kernels  122 us (99%)
    pallas_call x1, Pallas kernels, body(): pl.pallas_call(kernel, out_shape=(jax.ShapeDtypeStruct((2, shots, trace),...  121 us

profile of v6, /device:TPU:1, one launch (start us, length us, event | category | flops | bytes accessed | tf_op | source)
XLA Modules:
  0.0 123.1 jit_solution(1552138113424161442)
XLA Ops:
  0.6 120.8 %shard_map.122 = (f32[2,64,512]{2,1,0:T(8,128)}, f32[8,128]{1,0:T(8,128)}) custom-call(s32[1,32]{1,0:T(1,128)} %bitcast.15, s32[1,32]{1,0:T(1,128)} %bitcast.16, s32[8]{0:T(128)} %bitcast.17, s32[8]{0:T(128)} %slot_sm.1, s32[64]{0:T(128)} %shot_sm.1, f32[2,64]{1,0:T(2,128)} %bitcast.14, f32[32,2,64,128]{3,2,1,0:T(8,128)} %res_hbm.1, ...), custom_call_target="tpu_custom_call" | custom-call | tf_op jit(solution)/shard_map/pallas_call | solution.py:811
  121.4 1.7 %shard_map.123 = (f32[2,64,512]{2,1,0:T(8,128)}, f32[8,128]{1,0:T(8,128)}) custom-call(f32[2,64,512]{2,1,0:T(8,128)} %get-tuple-element.6.u_ref, f32[8,128]{1,0:T(8,128)} %get-tuple-element.7.model_ref), custom_call_target="tpu_custom_call" | custom-call | tf_op jit(solution)/shard_map/pallas_call | solution.py:899

commit v7 on v6

--- a/solution.py
+++ b/solution.py
@@ -463,10 +463,6 @@
         def _():
             up_copy(c, w).start()
 
-        @pl.when(has_leaf)
-        def _():
-            up_copy(c, w, True).start()
-
         if w == 0:
             back_copy(rows, h).start()
 
@@ -481,6 +477,10 @@
             @pl.when(lat < lats - 1)
             def _():
                 last_cells(rows, 1, h, after).start()
+
+        @pl.when(has_leaf)
+        def _():
+            up_copy(c, w, True).start()
 
     def down(c, carry):
         rows = rows_of(c)

time: 123 us -> 123 us (level)
  no operation moved by 1% of the time
where the time goes in v7:
time: 123 us
  Pallas kernels  122 us (99%)
    pallas_call x1, Pallas kernels, body(): pl.pallas_call(kernel, out_shape=(jax.ShapeDtypeStruct((2, shots, trace),...  121 us

profile of v7, /device:TPU:1, one launch (start us, length us, event | category | flops | bytes accessed | tf_op | source)
XLA Modules:
  0.0 123.1 jit_solution(7789218063813432684)
XLA Ops:
  0.6 120.8 %shard_map.122 = (f32[2,64,512]{2,1,0:T(8,128)}, f32[8,128]{1,0:T(8,128)}) custom-call(s32[1,32]{1,0:T(1,128)} %bitcast.15, s32[1,32]{1,0:T(1,128)} %bitcast.16, s32[8]{0:T(128)} %bitcast.17, s32[8]{0:T(128)} %slot_sm.1, s32[64]{0:T(128)} %shot_sm.1, f32[2,64]{1,0:T(2,128)} %bitcast.14, f32[32,2,64,128]{3,2,1,0:T(8,128)} %res_hbm.1, ...), custom_call_target="tpu_custom_call" | custom-call | tf_op jit(solution)/shard_map/pallas_call | solution.py:811
  121.4 1.7 %shard_map.123 = (f32[2,64,512]{2,1,0:T(8,128)}, f32[8,128]{1,0:T(8,128)}) custom-call(f32[2,64,512]{2,1,0:T(8,128)} %get-tuple-element.6.u_ref, f32[8,128]{1,0:T(8,128)} %get-tuple-element.7.model_ref), custom_call_target="tpu_custom_call" | custom-call | tf_op jit(solution)/shard_map/pallas_call | solution.py:899
